TPU v7x, 256 devices: a whole 4x4x8 slice. The times are simulated.
256 devices in a mesh: event: 8 (over x, z_lo), cuts: 32 (over z_hi, y, core).
Axes of the slice: x: 4, y: 4, z: 8 (z_hi: 4, z_lo: 2; z = z_hi * 2 + z_lo), core: 2. Of those that a mesh axis runs over, the one named last changes fastest.
Arguments:
- forward_displacement: float32 [8, 557568], P('event', 'cuts'), may hold values from -6 to 6
- forward_velocity: float32 [8, 557568], P('event', 'cuts'), may hold values from -6 to 6
- adjoint_displacement: float32 [8, 557568], P('event', 'cuts'), may hold values from -6 to 6
- adjoint_velocity: float32 [8, 557568], P('event', 'cuts'), may hold values from -6 to 6
- inverse_mass: float32 [557568], P('cuts'), may hold values from 0.3 to 3
- shear_modulus: float32 [125, 8192], P(None, 'cuts'), may hold values from 0.5 to 4
- connectivity: int32 [125, 8192], P(None, 'cuts'), may hold values from 0 to 18512, as said below
- face_points: int32 [32, 1152], P('cuts'), may hold values from 0 to 1088, as said below
- element_count: int32 [32], P('cuts'), may hold values from 128 to 256, as said below
Outputs:
- forward_displacement_next: float32 [8, 557568], P('event', 'cuts')
- forward_velocity_next: float32 [8, 557568], P('event', 'cuts')
- adjoint_displacement_next: float32 [8, 557568], P('event', 'cuts')
- adjoint_velocity_next: float32 [8, 557568], P('event', 'cuts')
- shear_kernel: float32 [512, 1089], P('cuts')
Inputs may be any that keep to these rules, and one draw needn't show every extreme that they name: `connectivity`: slot n of slice s is the element (ex, ey, ez) of a structured block of 4 x 8 x 8 elements, in an order drawn per slice; its point (i, j, k) has coordinates x = 4 ex + i, y = 4 ey + j, z = 4 ez + k and index x 1089 + y * 33 + z for x < 16; points with x = 16 lie on the next slice's first plane and have index 17424 + g, where g is their slot in the next slice's face list. `face_points`: row s lists in slots 0 to 1088 each point of slice s with x = 0 once; slots 1089 to 1151 hold 0. `element_count`: some slice has all 256 slots live in every draw.
All inputs are finite; a program needn't handle non-finite values.
Results may differ from a plain program's by a relative error of at most 0.0001.
Values sent between devices are 32-bit elements; how exact they have to be, the bound alone decides.
A program may use at most 128 MiB of HBM per device.

v0:
```python
import jax
import jax.numpy as jnp
import numpy as np
from jax import lax
from jax.sharding import PartitionSpec as P

NGLL = 5
PXU = 16
PY = 33
PZ = 33
PYZ = 1089
NPTS = 17424
NBUF = 1152


time_step = 0.02
cross_sigma = 1.5
cross_reach = 4


def from_behind(block, axis, distance):
    devices = range(lax.axis_size(axis))
    route = [((i - distance) % len(devices), i) for i in devices]
    return lax.ppermute(block, axis, route)


def with_halo(cells, sides, width):
    for axis, dim in sides:
        count = lax.axis_size(axis)
        head = lax.slice_in_dim(cells, 0, width, axis=dim)
        tail = lax.slice_in_dim(cells, cells.shape[dim] - width, cells.shape[dim], axis=dim)
        cells = jnp.concatenate(
            [
                lax.ppermute(tail, axis, [(i, (i + 1) % count) for i in range(count)]),
                cells,
                lax.ppermute(head, axis, [((i + 1) % count, i) for i in range(count)]),
            ],
            axis=dim,
        )
    return cells


def gll_tables():
    nodes = np.array([-1.0, -np.sqrt(3.0 / 7.0), 0.0, np.sqrt(3.0 / 7.0), 1.0])
    quad_weights = np.array([0.1, 49.0 / 90.0, 32.0 / 45.0, 49.0 / 90.0, 0.1])
    barycentric = np.array(
        [
            1.0
            / np.prod(
                [
                    nodes[node_row] - nodes[node_column]
                    for node_column in range(5)
                    if node_column != node_row
                ]
            )
            for node_row in range(5)
        ]
    )
    derivative = np.zeros((5, 5))
    for node_row in range(5):
        for node_column in range(5):
            if node_column != node_row:
                derivative[node_row, node_column] = (
                    barycentric[node_column]
                    / barycentric[node_row]
                    / (nodes[node_row] - nodes[node_column])
                )
        derivative[node_row, node_row] = -np.sum(derivative[node_row])
    weights_cube = (
        quad_weights[:, None, None] * quad_weights[None, :, None] * quad_weights[None, None, :]
    ).reshape(125)
    return (
        jnp.asarray(derivative, dtype=jnp.float32),
        jnp.asarray(weights_cube, dtype=jnp.float32),
    )


def gradients(cube, derivative):
    grad_x = jnp.einsum("il,ljkn->ijkn", derivative, cube, precision=lax.Precision.HIGHEST)
    grad_y = jnp.einsum("jl,ilkn->ijkn", derivative, cube, precision=lax.Precision.HIGHEST)
    grad_z = jnp.einsum("kl,ijln->ijkn", derivative, cube, precision=lax.Precision.HIGHEST)
    return (grad_x, grad_y, grad_z)


def stiffness(grads, flux_cube, derivative):
    term_x = jnp.einsum(
        "li,ljkn->ijkn", derivative, flux_cube * grads[0], precision=lax.Precision.HIGHEST
    )
    term_y = jnp.einsum(
        "lj,ilkn->ijkn", derivative, flux_cube * grads[1], precision=lax.Precision.HIGHEST
    )
    term_z = jnp.einsum(
        "lk,ijln->ijkn", derivative, flux_cube * grads[2], precision=lax.Precision.HIGHEST
    )
    return -(term_x + term_y + term_z)


def along_weight(offset):
    sigma = PXU / 4.0
    return jnp.exp(-offset * offset / (2.0 * sigma * sigma))


def along_band():
    offsets = jnp.arange(-PXU, PXU + 1, dtype=jnp.int32).astype(jnp.float32)
    norm_total = jnp.sum(along_weight(offsets))
    row_index = jnp.arange(PXU, dtype=jnp.int32)
    rim_index = jnp.arange(3 * PXU, dtype=jnp.int32)
    spread = rim_index[None, :] - PXU - row_index[:, None]
    inside = (jnp.abs(spread) <= PXU).astype(jnp.float32)
    return along_weight(spread.astype(jnp.float32)) * inside / norm_total


def cross_matrix(count):
    point_index = jnp.arange(count, dtype=jnp.int32)
    offset = (point_index[:, None] - point_index[None, :]).astype(jnp.float32)
    kept = jnp.exp(-offset * offset / (2.0 * cross_sigma * cross_sigma)) * (
        jnp.abs(offset) <= cross_reach
    ).astype(jnp.float32)
    return kept / jnp.sum(kept, axis=1, keepdims=True)


def on_device(
    forward_displacement,
    forward_velocity,
    adjoint_displacement,
    adjoint_velocity,
    inverse_mass,
    shear_modulus,
    connectivity,
    face_points,
    element_count,
):
    derivative, weights_cube = gll_tables()
    faces = face_points[0]
    elements = connectivity.shape[1]
    active = (jnp.arange(elements, dtype=jnp.int32) < element_count[0]).astype(jnp.float32)
    flux = weights_cube[:, None] * shear_modulus * active[None, :]
    flux_cube = flux.reshape(NGLL, NGLL, NGLL, elements)
    forward_now = forward_displacement[0]
    adjoint_now = adjoint_displacement[0]
    both_now = jnp.stack([forward_now, adjoint_now])
    both_ghost = from_behind(both_now[:, faces], "cuts", -1)
    both_ext = jnp.concatenate([both_now, both_ghost], axis=1)
    gathered = both_ext[:, connectivity]
    cubes = gathered.transpose(1, 0, 2).reshape(NGLL, NGLL, NGLL, 2 * elements)
    both_grads = gradients(cubes, derivative)
    both_flux = jnp.concatenate([flux_cube, flux_cube], axis=3)
    both_force = stiffness(both_grads, both_flux, derivative)
    forward_term = both_force[..., :elements]
    adjoint_term = both_force[..., elements:]
    product = (
        both_grads[0][..., :elements] * both_grads[0][..., elements:]
        + both_grads[1][..., :elements] * both_grads[1][..., elements:]
        + both_grads[2][..., :elements] * both_grads[2][..., elements:]
    )
    kernel_term = -flux_cube * product
    stacked_terms = jnp.stack(
        [forward_term.reshape(-1), adjoint_term.reshape(-1), kernel_term.reshape(-1)], axis=1
    )
    point_ids = connectivity.reshape(-1)
    total = NPTS + NBUF
    summed_terms = jax.ops.segment_sum(stacked_terms, point_ids, num_segments=total)
    forward_force = summed_terms[:, 0]
    adjoint_force = summed_terms[:, 1]
    kernel_ext = summed_terms[:, 2]
    back_forward, back_adjoint, back_kernel = from_behind(
        (forward_force[NPTS:], adjoint_force[NPTS:], kernel_ext[NPTS:]), "cuts", 1
    )
    forward_force = forward_force[:NPTS].at[faces].add(back_forward)
    adjoint_force = adjoint_force[:NPTS].at[faces].add(back_adjoint)
    kernel_points = kernel_ext[:NPTS].at[faces].add(back_kernel)
    forward_speed_next = forward_velocity[0] - time_step * inverse_mass * forward_force
    forward_now_next = forward_now - time_step * forward_speed_next
    adjoint_speed_next = adjoint_velocity[0] + time_step * inverse_mass * adjoint_force
    adjoint_now_next = adjoint_now + time_step * adjoint_speed_next
    event_kernel = kernel_points.reshape(PXU, PYZ)
    band = along_band()
    cross = jnp.kron(cross_matrix(PY), cross_matrix(PZ))
    summed = lax.psum(event_kernel, "event")
    rimmed = with_halo(summed, (("cuts", 0),), PXU)
    smoothed_along = jnp.dot(band, rimmed, precision=lax.Precision.HIGHEST)
    shear_kernel = jnp.dot(smoothed_along, cross.T, precision=lax.Precision.HIGHEST)
    return (
        forward_now_next[None, :],
        forward_speed_next[None, :],
        adjoint_now_next[None, :],
        adjoint_speed_next[None, :],
        shear_kernel,
    )


def solution(mesh):
    in_specs = (
        P("event", "cuts"),
        P("event", "cuts"),
        P("event", "cuts"),
        P("event", "cuts"),
        P("cuts"),
        P(None, "cuts"),
        P(None, "cuts"),
        P("cuts", None),
        P("cuts"),
    )
    out_specs = (
        P("event", "cuts"),
        P("event", "cuts"),
        P("event", "cuts"),
        P("event", "cuts"),
        P("cuts", None),
    )
    return jax.shard_map(
        on_device, mesh=mesh, in_specs=in_specs, out_specs=out_specs, check_vma=False
    )
```

profile of v0, /device:TPU:1, one launch (start us, length us, event | category | flops | bytes accessed | tf_op | source)
XLA Modules:
  0.0 432.9 jit_solution(18053370572969491955)
XLA Ops:
  7.2 0.7 fusion.35
  8.0 1.1 pad_maximum_fusion.2
  9.1 5.1 %copy.95 = f32[2,17424]{0,1:T(8,128)} copy(f32[2,17424]{1,0:T(2,128)S(1)} %pad_maximum_fusion.2) | data formatting | bytes 278784 | tf_op jit(solution)/shard_map/stack | solution.py:141
  14.1 6.0 %gather_fusion = f32[1152,2]{1,0:T(8,128)S(1)} fusion(f32[2,17424]{0,1:T(8,128)} %copy.95, s32[2048]{0:T(1024)S(1)} %pad_clamp_fusion.1), kind=kCustom, calls=%fused_computation | custom fusion | bytes 23040 | tf_op jit(solution)/shard_map/gather | solution.py:142
  20.3 3.3 collective-permute-start
  24.7 8.9 %broadcast_multiply_fusion = f32[33,33,33,33]{3,2,1,0:T(8,128)} fusion(f32[33,33]{1,0:T(8,128)S(1)} %fusion.25), kind=kLoop, calls=%fused_computation.6 | loop fusion | flops 1185921 | bytes 4748040 | tf_op jit(solution)/shard_map/jit(kron)/mul | solution.py:178
  33.8 5.3 %copy.97 = f32[2,18576]{0,1:T(8,128)} copy(f32[2,18576]{1,0:T(2,128)S(1)} %pad_maximum_fusion.1) | data formatting | bytes 297216 | tf_op jit(solution)/shard_map/concatenate | solution.py:143
  39.2 63.0 %gather_fusion.1 = f32[32000,2]{1,0:T(8,128)} fusion(f32[2,18576]{0,1:T(8,128)} %copy.97, s32[32768]{0:T(1024)S(1)} %pad_clamp_fusion), kind=kCustom, calls=%fused_computation.1 | custom fusion | bytes 640000 | tf_op jit(solution)/shard_map/gather | solution.py:144
  102.1 9.1 %copy.98 = f32[125,2,256]{2,1,0:T(2,128)S(1)} copy(f32[125,2,256]{1,2,0:T(8,128)} %bitcast.37) | data formatting | bytes 512000 | tf_op jit(solution)/shard_map/transpose | solution.py:145
  114.0 0.6 fusion.4
  114.6 0.6 fusion.6
  115.3 0.8 fusion.3
  117.1 8.5 %copy.114 = f32[32000,3]{1,0:T(8,128)} copy(f32[32000,3]{0,1:T(4,128)S(1)} %pad_maximum_fusion) | data formatting | bytes 768000 | tf_op jit(solution)/shard_map/stack | solution.py:157
  125.6 176.6 %scatter_custom_fusion = f32[18576,3]{1,0:T(8,128)} fusion(s32[32000]{0:T(1024)S(1)} %reshape.155, f32[32000,3]{1,0:T(8,128)} %copy.114, f32[]{:T(128)} %constant.13.clone.1), kind=kCustom, calls=%fused_computation.10 | custom fusion | flops 96000 | bytes 223424 | tf_op jit(solution)/shard_map/scatter-add | solution.py:162
  302.2 2.5 slice_reduce_fusion.3
  304.8 16.4 %slice_reduce_fusion = (f32[17424]{0:T(1024)S(1)}, f32[17424]{0:T(1024)S(1)}, f32[17424]{0:T(1024)S(1)}) fusion(f32[18576,3]{1,0:T(8,128)} %scatter_custom_fusion), kind=kLoop, calls=%fused_computation.7 | loop fusion | bytes 418176 | tf_op jit(solution)/shard_map/slice | solution.py:171
  321.3 1.1 collective-permute-start.2
  322.4 8.8 %scatter_fusion.2 = f32[17424]{0:T(1024)S(1)} fusion(f32[17424]{0:T(1024)S(1)} %get-tuple-element.8, s32[1152]{0:T(1024)S(1)} %fusion.35, f32[1152]{0:T(1024)S(1)} %collective-permute-done.3), kind=kCustom, calls=%fused_computation.5 | custom fusion | flops 1152 | bytes 18432 | tf_op jit(solution)/shard_map/scatter-add | solution.py:171
  331.2 0.7 reshape.136
  332.4 15.5 %mul.130 = f32[1089,1089]{1,0:T(8,128)} reshape(f32[33,33,33,33]{3,2,1,0:T(8,128)} %broadcast_multiply_fusion) | data formatting | bytes 9487368 | tf_op jit(solution)/shard_map/jit(kron)/mul | solution.py:178
  348.3 0.7 fusion.43
  349.0 8.8 %scatter_fusion = f32[17424]{0:T(1024)S(1)} fusion(f32[17424]{0:T(1024)S(1)} %get-tuple-element.10, s32[1152]{0:T(1024)S(1)} %fusion.35, f32[1152]{0:T(1024)S(1)} %collective-permute-done.1), kind=kCustom, calls=%fused_computation.3 | custom fusion | flops 1152 | bytes 18432 | tf_op jit(solution)/shard_map/scatter-add | solution.py:169
  357.8 9.0 %scatter_fusion.1 = f32[17424]{0:T(1024)S(1)} fusion(f32[17424]{0:T(1024)S(1)} %get-tuple-element.9, s32[1152]{0:T(1024)S(1)} %fusion.35, f32[1152]{0:T(1024)S(1)} %collective-permute-done.2), kind=kCustom, calls=%fused_computation.4 | custom fusion | flops 1152 | bytes 18432 | tf_op jit(solution)/shard_map/scatter-add | solution.py:170
  366.8 39.9 %all-reduce.2.cloned.1.call-done = f32[16,1089]{1,0:T(8,128)} async-done(((f32[16,1089]{1,0:T(8,128)}), f32[16,1089]{1,0:T(8,128)}) %all-reduce.2.cloned.1.call-update) | async-done | bytes 69712 | tf_op jit(solution)/shard_map/psum | solution.py:179
  406.7 6.3 %collective-permute-start.4 = (f32[16,1089]{1,0:T(8,128)}, f32[16,1089]{1,0:T(8,128)S(1)}, u32[]{:S(2)}, u32[]{:S(2)}) collective-permute-start(f32[16,1089]{1,0:T(8,128)} %all-reduce.2.cloned.1.call-done), channel_id=1, source_target_pairs={{0,1},{1,2},{2,3},{3,4},{4,5},{5,6},{6,7},{7,8},{8,9},{9,10},{10,1... | collective-permute-start | bytes 209096 | tf_op jit(solution)/shard_map/ppermute | solution.py:34
  413.1 0.7 broadcast_in_dim.16
  413.8 0.7 broadcast_in_dim.17
  414.4 0.7 broadcast_in_dim.20
  415.1 0.7 broadcast_in_dim.21
  415.8 1.2 collective-permute-done.5
  417.0 1.8 fusion.13
  418.8 7.3 %fusion.52 = f32[16,1089]{1,0:T(8,128)} fusion(f32[16,1089]{1,0:T(8,128)S(1)} %fusion.13, f32[1089,1089]{1,0:T(8,128)} %mul.130), kind=kOutput, calls=%fused_computation.91 | convolution fusion | flops 227696832 | bytes 4883076 | tf_op jit(solution)/shard_map/dot_general | solution.py:182
  (63 shorter events, 5.4 us)
Async XLA Ops:
  7.2 17.3 %copy-start.8 = (f32[125]{0:T(128)S(1)}, f32[125]{0:T(128)}, u32[]{:S(2)}) copy-start(f32[125]{0:T(128)} %constant.35.clone) | copy-start | bytes 1504
  7.2 16.5 %copy-start.2 = (s32[125,256]{1,0:T(8,128)S(1)}, s32[125,256]{1,0:T(8,128)}, u32[]{:S(2)}) copy-start(s32[125,256]{1,0:T(8,128)} %param.17) | copy-start | bytes 384004
  7.2 17.3 %copy-start.4 = (f32[125,256]{1,0:T(8,128)S(1)}, f32[125,256]{1,0:T(8,128)}, u32[]{:S(2)}) copy-start(f32[125,256]{1,0:T(8,128)} %param.16) | copy-start | bytes 384004
  7.2 399.5 %all-reduce.2.cloned.1.call-start = ((), (), s32[]{:S(2)}) async-start(), calls=%async_computation | async-start | bytes 147456 | tf_op jit(solution)/shard_map/psum | solution.py:179
  20.3 13.4 %collective-permute-start = (f32[2,1152]{1,0:T(2,128)S(1)}, f32[2,1152]{1,0:T(2,128)S(1)}, u32[]{:S(2)}, u32[]{:S(2)}) collective-permute-start(f32[2,1152]{1,0:T(2,128)S(1)} %copy.96), channel_id=1, source_target_pairs={{1,0},{2,1},{3,2},{4,3},{5,4},{6,5},{7,6},{8,7},{9,8},{10,9},{11,1... | collective-permute-start | bytes 27656 | tf_op jit(solution)/shard_map/ppermute | solution.py:24
  24.7 9.0 %copy-start = (f32[1,17424]{1,0:T(1,128)S(1)}, f32[1,17424]{1,0:T(1,128)}, u32[]{:S(2)}) copy-start(f32[1,17424]{1,0:T(1,128)} %param.11) | copy-start | bytes 209092
  24.7 9.0 %copy-start.1 = (f32[1,17424]{1,0:T(1,128)S(1)}, f32[1,17424]{1,0:T(1,128)}, u32[]{:S(2)}) copy-start(f32[1,17424]{1,0:T(1,128)} %param.13) | copy-start | bytes 209092
  39.2 72.3 %copy-start.3 = (f32[5,5,1,1]{1,0,3,2:T(8,128)S(1)}, f32[5,5,1,1]{1,0,3,2:T(8,128)}, u32[]{:S(2)}) copy-start(f32[5,5,1,1]{1,0,3,2:T(8,128)} %constant.43) | copy-start | bytes 304
  304.7 17.7 %collective-permute-start.3 = (f32[1152]{0:T(1024)S(1)}, f32[1152]{0:T(1024)S(1)}, u32[]{:S(2)}, u32[]{:S(2)}) collective-permute-start(f32[1152]{0:T(1024)S(1)} %get-tuple-element.5), channel_id=1, source_target_pairs={{31,0},{0,1},{1,2},{2,3},{3,4},{4,5},{5,6},{6,7},{7,8},{8,9},{9,10... | collective-permute-start | bytes 13832 | tf_op jit(solution)/shard_map/ppermute | solution.py:24
  321.2 27.8 %collective-permute-start.1 = (f32[1152]{0:T(1024)S(1)}, f32[1152]{0:T(1024)S(1)}, u32[]{:S(2)}, u32[]{:S(2)}) collective-permute-start(f32[1152]{0:T(1024)S(1)} %get-tuple-element.7), channel_id=1, source_target_pairs={{31,0},{0,1},{1,2},{2,3},{3,4},{4,5},{5,6},{6,7},{7,8},{8,9},{9,10... | collective-permute-start | bytes 13832 | tf_op jit(solution)/shard_map/ppermute | solution.py:24
  321.3 36.5 %collective-permute-start.2 = (f32[1152]{0:T(1024)S(1)}, f32[1152]{0:T(1024)S(1)}, u32[]{:S(2)}, u32[]{:S(2)}) collective-permute-start(f32[1152]{0:T(1024)S(1)} %get-tuple-element.6), channel_id=1, source_target_pairs={{31,0},{0,1},{1,2},{2,3},{3,4},{4,5},{5,6},{6,7},{7,8},{8,9},{9,10... | collective-permute-start | bytes 13832 | tf_op jit(solution)/shard_map/ppermute | solution.py:24
  332.3 15.6 %copy-start.6 = (f32[1,17424]{1,0:T(1,128)S(1)}, f32[1,17424]{1,0:T(1,128)}, u32[]{:S(2)}) copy-start(f32[1,17424]{1,0:T(1,128)} %param.12) | copy-start | bytes 209092
  332.4 15.7 %copy-start.7 = (f32[1,17424]{1,0:T(1,128)S(1)}, f32[1,17424]{1,0:T(1,128)}, u32[]{:S(2)}) copy-start(f32[1,17424]{1,0:T(1,128)} %param.14) | copy-start | bytes 209092
  357.8 55.3 %copy-start.5 = (f32[17424]{0:T(1024)S(1)}, f32[17424]{0:T(1024)}, u32[]{:S(2)}) copy-start(f32[17424]{0:T(1024)} %param.15) | copy-start | bytes 209092
  406.7 9.1 %collective-permute-start.4 = (f32[16,1089]{1,0:T(8,128)}, f32[16,1089]{1,0:T(8,128)S(1)}, u32[]{:S(2)}, u32[]{:S(2)}) collective-permute-start(f32[16,1089]{1,0:T(8,128)} %all-reduce.2.cloned.1.call-done), channel_id=1, source_target_pairs={{0,1},{1,2},{2,3},{3,4},{4,5},{5,6},{6,7},{7,8},{8,9},{9,10},{10,1... | collective-permute-start | bytes 209096 | tf_op jit(solution)/shard_map/ppermute | solution.py:34
  413.0 4.0 collective-permute-start.5
Sparse Core Ops, SparseCore 0:
  332.1 74.5 all-reduce.1
where the time goes:
time: 437 us; the launch traced here: 433 us
  other arithmetic  217 us (50%)
  local copies, waits for them, and re-layouts  136 us (31%)
  waiting for transfers between devices  41.1 us (9%)
  between operations  15.1 us (3%)
  matrix products  12.8 us (3%)
  starting transfers between devices  11 us (3%)
    scatter-add x1, other arithmetic, on_device(): jax.ops.segment_sum(stacked_terms, point_ids, num_segments=total)  177 us
    gather x1, local copies, waits for them, and re-layouts, on_device(): gathered = both_ext[:, connectivity]  63 us
    psum x1, waiting for transfers between devices, on_device(): summed = lax.psum(event_kernel, 'event')  39.9 us
    slice x1, local copies, waits for them, and re-layouts, on_device(): kernel_points = kernel_ext[:NPTS].at[faces].add(back_kernel)  16.4 us
    mul x1, local copies, waits for them, and re-layouts, on_device(): cross = jnp.kron(cross_matrix(PY), cross_matrix(PZ))  15.5 us
    transpose x1, local copies, waits for them, and re-layouts, on_device(): cubes = gathered.transpose(1, 0, 2).reshape(NGLL, NGLL, NGLL, 2 * elements)  9.08 us
    scatter-add x1, other arithmetic, on_device(): adjoint_force = adjoint_force[:NPTS].at[faces].add(back_adjoint)  9.03 us
    mul x1, other arithmetic, on_device(): cross = jnp.kron(cross_matrix(PY), cross_matrix(PZ))  8.92 us
  transfers between devices with their start and end apart: 7, of which 2 were waited for; matrix products, arithmetic and copies ran while one was open for 17% of the time, Pallas kernels for 0%

commit v1 on v0

v1 whole, which is shorter than its diff:
```python
import functools

import jax
import jax.numpy as jnp
import numpy as np
from jax import lax
from jax.experimental import pallas as pl
from jax.experimental.pallas import tpu as pltpu
from jax.sharding import PartitionSpec as P

NGLL = 5
PXU = 16
PY = 33
PZ = 33
PYZ = 1089
NPTS = 17424
LANES = 1152

time_step = 0.02
cross_sigma = 1.5
cross_reach = 4

MESH = pl.DeviceIdType.MESH


def gll_tables():
    nodes = np.array([-1.0, -np.sqrt(3.0 / 7.0), 0.0, np.sqrt(3.0 / 7.0), 1.0])
    quad = np.array([0.1, 49.0 / 90.0, 32.0 / 45.0, 49.0 / 90.0, 0.1])
    bary = np.array(
        [1.0 / np.prod([nodes[a] - nodes[b] for b in range(5) if b != a]) for a in range(5)]
    )
    deriv = np.zeros((5, 5))
    for a in range(5):
        for b in range(5):
            if b != a:
                deriv[a, b] = bary[b] / bary[a] / (nodes[a] - nodes[b])
        deriv[a, a] = -np.sum(deriv[a])
    cube = (quad[:, None, None] * quad[None, :, None] * quad[None, None, :]).reshape(125)
    return deriv.astype(np.float32), cube.astype(np.float32)


DERIV, CUBE = gll_tables()
D = [[float(DERIV[a, b]) for b in range(5)] for a in range(5)]


def lane_tables():
    lane = np.arange(LANES)
    live = lane < PYZ
    y, z = lane // PZ, lane % PZ
    rows = []
    for pos, extent in ((y, PY), (z, PZ)):
        for d in range(-3, 5):
            node = pos % 4
            inside = live & (pos < extent - 1) & (node + d >= 0) & (node + d <= 4)
            value = DERIV[node, np.clip(node + d, 0, 4)]
            rows.append(np.where(inside, value, 0.0))
    for pos, extent in ((y, PY), (z, PZ)):
        weight = lambda d: np.exp(-d * d / (2.0 * cross_sigma * cross_sigma))
        norm = np.zeros(LANES)
        for d in range(-cross_reach, cross_reach + 1):
            norm += np.where((pos + d >= 0) & (pos + d < extent), weight(d), 0.0)
        for d in range(-cross_reach, cross_reach + 1):
            inside = live & (pos + d >= 0) & (pos + d < extent)
            rows.append(np.where(inside, weight(d) / norm, 0.0))
    rows = np.stack(rows).astype(np.float32)
    return np.pad(rows, ((0, 56 - rows.shape[0]), (0, 0)))


def band_table(events):
    sigma = PXU / 4.0
    w = lambda d: np.exp(-d * d / (2.0 * sigma * sigma))
    norm = np.sum(w(np.arange(-PXU, PXU + 1).astype(np.float64)))
    chunk = PXU // events
    table = np.zeros((events, 3, chunk, PXU))
    for e in range(events):
        for o in range(3):
            for r in range(chunk):
                gap = 16 * (o - 1) + chunk * e + r - np.arange(PXU)
                table[e, o, r] = np.where(np.abs(gap) <= PXU, w(gap.astype(np.float64)) / norm, 0.0)
    table = table.reshape(events * 3 * chunk, 4, 4).transpose(0, 2, 1)
    table = np.stack([table, np.zeros_like(table)], axis=2)
    return table.reshape(events * 3 * chunk, 2 * PXU).astype(np.float32)


def shifted(x, step):
    shift = (-step) % LANES
    return x if shift == 0 else pltpu.roll(x, shift, 1)


def stencil(u, coef_ref, base, stride):
    main = end = None
    for d in range(-4, 5):
        moved = shifted(u, stride * d)
        if d >= -3:
            row = base + d + 3
            term = coef_ref[row : row + 1, :] * moved
            main = term if main is None else main + term
        if d <= 0:
            term = D[4][4 + d] * moved
            end = term if end is None else end + term
    return main, end


def spread(fm, fe, coef_ref, base, stride):
    total = None
    for d in range(-4, 5):
        term = None
        if d >= -3:
            row = base + d + 3
            term = coef_ref[row : row + 1, :] * fm
        if d <= 0:
            part = D[4][4 + d] * fe
            term = part if term is None else term + part
        term = shifted(term, -stride * d)
        total = term if total is None else total + term
    return total


def step_kernel(
    events,
    slices,
    u_ref,
    v_ref,
    mass_ref,
    lhs_ref,
    base_ref,
    coef_ref,
    band_ref,
    un_ref,
    vn_ref,
    sk_ref,
    placed,
    ax,
    aym,
    aye,
    azm,
    aze,
    ghost,
    tail_u,
    tail_a,
    stage_g,
    stage_u,
    stage_a,
    force,
    kern,
    part,
    recv,
    rows,
    halo_send,
    halo_recv,
    part_send,
    part_recv,
    rows_send,
    rows_recv,
):
    chunk = PXU // events
    others = 3 * events - 1
    e = lax.axis_index("event")
    s = lax.axis_index("cuts")
    ahead, behind = lax.rem(s + 1, slices), lax.rem(s + slices - 1, slices)

    def partner(m):
        step = lax.rem(m + 1, 3)
        return {
            "event": lax.rem(e + (m + 1) // 3, events),
            "cuts": lax.rem(s + step + jnp.where(step == 2, slices - 3, 0), slices),
        }

    barrier = pltpu.get_barrier_semaphore()

    def greet(m, carry):
        pl.semaphore_signal(barrier, inc=1, device_id=partner(m), device_id_type=MESH)
        return carry

    lax.fori_loop(0, others, greet, 0)

    for f in range(2):
        stage_g[f : f + 1, :] = u_ref[4 * f : 4 * f + 1, :]
        for i in range(4):
            at = 8 * i + 4 * f + 3
            stage_u[2 * i + f : 2 * i + f + 1, :] = u_ref[at : at + 1, :]

    lhs = lhs_ref[...]
    hi = lhs.astype(jnp.bfloat16)
    rest = lhs - hi.astype(jnp.float32)
    mid = rest.astype(jnp.bfloat16)
    low = (rest - mid.astype(jnp.float32)).astype(jnp.bfloat16)
    lane = lax.broadcasted_iota(jnp.int32, (256, LANES), 1)
    pick = jnp.where(base_ref[...] == lane, 1.0, 0.0).astype(jnp.bfloat16)
    placed[...] = (
        jnp.dot(hi, pick, preferred_element_type=jnp.float32)
        + jnp.dot(mid, pick, preferred_element_type=jnp.float32)
        + jnp.dot(low, pick, preferred_element_type=jnp.float32)
    )

    pl.semaphore_wait(barrier, others)
    to_behind = pltpu.make_async_remote_copy(
        stage_g, ghost, halo_send.at[0], halo_recv.at[0], {"cuts": behind}, MESH
    )
    to_behind.start()
    to_ahead = pltpu.make_async_remote_copy(
        stage_u, tail_u, halo_send.at[1], halo_recv.at[1], {"cuts": ahead}, MESH
    )
    to_ahead.start()

    twice = lambda x: jnp.concatenate([x, x], axis=0)
    row = lax.broadcasted_iota(jnp.int32, (8, LANES), 0)
    kinds = (aym, aye, azm, aze)
    for c in (2, 0, 1):
        sums = [None] * 4
        for j in range(5):
            for k in range(5):
                first = 24 * (5 * j + k) + 8 * c
                moved = shifted(placed[first : first + 8, :], -(PZ * j + k))
                q = 2 * (j == 4) + (k == 4)
                sums[q] = moved if sums[q] is None else sums[q] + moved
        mm, me, em, ee = sums
        whole = (mm + me) + (em + ee)
        pairs = (mm + me, em + ee, mm + em, me + ee)
        if c == 2:
            ax[32:40, :] = twice(whole[0:4, :])
            for q in range(4):
                stage_a[4 + q : 5 + q, :] = sums[q][3:4, :]
                shifted_layer = pltpu.roll(twice(pairs[q][0:4, :]), 1, 0)
                kinds[q][0:8, :] = jnp.where(row % 4 == 0, 0.0, shifted_layer)
        else:
            for half in range(2):
                i = 2 * c + half
                some = slice(4 * half, 4 * half + 4)
                ax[8 * i : 8 * i + 8, :] = twice(whole[some, :])
                stage_a[i : i + 1, :] = whole[4 * half + 3 : 4 * half + 4, :]
                for q in range(4):
                    value = twice(pairs[q][some, :])
                    if i == 0:
                        value = value + kinds[q][0:8, :]
                    kinds[q][8 * i : 8 * i + 8, :] = value

    flux_ahead = pltpu.make_async_remote_copy(
        stage_a, tail_a, halo_send.at[2], halo_recv.at[2], {"cuts": ahead}, MESH
    )
    flux_ahead.start()

    for i in (1, 2, 3, 0):
        at = 8 * i
        if i == 0:
            flux_ahead.wait()
            mm, me, em, ee = (tail_a[4 + q : 5 + q, :] for q in range(4))
            for ref, value in zip(kinds, (mm + me, em + ee, mm + em, me + ee)):
                ref[0:1, :] += value
                ref[4:5, :] += value
        u = u_ref[at : at + 8, :]
        ksum = tsum = None
        for base, stride, m_ref, e_ref in ((0, PZ, aym, aye), (8, 1, azm, aze)):
            gm, ge = stencil(u, coef_ref, base, stride)
            fm, fe = m_ref[at : at + 8, :] * gm, e_ref[at : at + 8, :] * ge
            term = fm * pltpu.roll(gm, 4, 0) + fe * pltpu.roll(ge, 4, 0)
            ksum = term if ksum is None else ksum + term
            term = spread(fm, fe, coef_ref, base, stride)
            tsum = term if tsum is None else tsum + term
        kern[at : at + 8, :] = ksum
        force[at : at + 8, :] = tsum

    to_behind.wait()
    to_ahead.wait()
    slab = [u_ref[8 * i : 8 * i + 8, :] for i in range(4)]
    last = pltpu.roll(slab[0], 7, 0)
    last = jnp.where(row == 3, ghost[0:1, :], jnp.where(row == 7, ghost[1:2, :], last))
    slab.append(last)
    grads = []
    for a in range(5):
        total = None
        for b in range(5):
            term = D[a][b] * slab[b]
            total = term if total is None else total + term
        grads.append(total)
    moved = [ax[8 * a : 8 * a + 8, :] * grads[a] for a in range(5)]
    prods = [moved[a] * pltpu.roll(grads[a], 4, 0) for a in range(5)]
    turned = []
    for a in range(5):
        total = None
        for b in range(5):
            term = D[b][a] * moved[b]
            total = term if total is None else total + term
        turned.append(total)
    edge = [tail_u[2 * i : 2 * i + 2, :] for i in range(4)] + [stage_g[...]]
    edge_flux = [tail_a[i : i + 1, :] for i in range(4)]
    edge_flux.append(
        (tail_a[4:5, :] + tail_a[5:6, :]) + (tail_a[6:7, :] + tail_a[7:8, :])
    )
    edge_force = edge_kern = None
    for a in range(5):
        total = None
        for b in range(5):
            term = D[a][b] * edge[b]
            total = term if total is None else total + term
        term = (D[a][4] * edge_flux[a]) * total
        edge_force = term if edge_force is None else edge_force + term
        if a == 4:
            edge_kern = edge_flux[4] * total[0:1, :] * total[1:2, :]

    back = pltpu.roll(turned[4], 1, 0)
    back = jnp.where(row == 0, edge_force[0:1, :], jnp.where(row == 4, edge_force[1:2, :], back))
    turned[0] = turned[0] + back
    back = pltpu.roll(prods[4], 1, 0)
    back = jnp.where(row == 0, edge_kern, back)
    prods[0] = prods[0] + back
    for i in range(4):
        kern[8 * i : 8 * i + 8, :] += prods[i]
        force[8 * i : 8 * i + 8, :] += turned[i]

    added = jnp.dot(
        -band_ref[...],
        kern[...],
        precision=lax.Precision.HIGHEST,
        preferred_element_type=jnp.float32,
    )
    for m in range(3 * events):
        part[m] = added[chunk * m : chunk * m + chunk, :]

    def spray(m, carry):
        step = lax.rem(m + 1, 3)
        to = partner(m)
        slot = 3 * to["event"] + lax.rem(step + 1, 3)
        pltpu.make_async_remote_copy(
            part.at[slot], recv.at[m], part_send, part_recv, to, MESH
        ).start()
        return carry

    lax.fori_loop(0, others, spray, 0)

    for i in range(4):
        at = slice(8 * i, 8 * i + 8)
        step = jnp.where(row < 4, time_step, -time_step)
        speed = v_ref[at, :] + (step * mass_ref[at, :]) * force[at, :]
        vn_ref[at, :] = speed
        un_ref[at, :] = u_ref[at, :] - step * speed

    pltpu.make_async_copy(recv, recv, part_recv).wait()
    total = part[3 * e + 1]
    for m in range(others):
        total = total + recv[m]
    across = None
    for d in range(-cross_reach, cross_reach + 1):
        term = coef_ref[20 + d : 21 + d, :] * shifted(total, PZ * d)
        across = term if across is None else across + term
    total, across = across, None
    for d in range(-cross_reach, cross_reach + 1):
        term = coef_ref[29 + d : 30 + d, :] * shifted(total, d)
        across = term if across is None else across + term
    rows[e] = across

    def share(m, carry):
        to = {"event": lax.rem(e + m + 1, events)}
        pltpu.make_async_remote_copy(
            rows.at[e], rows.at[e], rows_send, rows_recv, to, MESH
        ).start()
        return carry

    lax.fori_loop(0, events - 1, share, 0)
    pltpu.make_async_copy(recv, recv, part_send).wait()
    some = rows.at[pl.ds(0, events - 1)]
    pltpu.make_async_copy(some, some, rows_recv).wait()
    pltpu.make_async_copy(some, some, rows_send).wait()
    for m in range(events):
        sk_ref[chunk * m : chunk * m + chunk, :] = rows[m]


def on_device(events, slices):
    def run(fd, fv, ad, av, inverse_mass, shear, connectivity, face_points, count):
        chunk = PXU // events
        layers = lambda x: jnp.pad(x.reshape(4, 4, PYZ), ((0, 0), (0, 0), (0, LANES - PYZ)))
        pair = lambda x, y: jnp.stack([layers(x), layers(y)]).transpose(2, 0, 1, 3).reshape(32, LANES)
        u = pair(fd[0], ad[0])
        v = pair(fv[0], av[0])
        mass = pair(inverse_mass, inverse_mass)
        first = connectivity[0]
        layer = first // (4 * PYZ)
        base = (first - 4 * PYZ * layer).reshape(256, 1)
        active = (jnp.arange(256, dtype=jnp.int32) < count[0]).astype(jnp.float32)
        flux = jnp.asarray(CUBE)[:, None] * shear * active[None, :]
        own = (layer[None, :] == jnp.arange(4, dtype=jnp.int32)[:, None]).astype(jnp.float32)
        cube = flux.reshape(5, 25, 256).transpose(1, 0, 2)
        lhs = (cube[:, :, None, :] * own[None, None, :, :]).reshape(25, 20, 256)
        lhs = jnp.pad(lhs, ((0, 0), (0, 4), (0, 0))).reshape(600, 256)
        vmem = pl.BlockSpec(memory_space=pltpu.VMEM)
        shape = jax.ShapeDtypeStruct
        f32 = jnp.float32
        big = lambda *dims: pltpu.VMEM((*dims, LANES), f32)
        un, vn, sk = pl.pallas_call(
            functools.partial(step_kernel, events, slices),
            out_shape=(shape((32, LANES), f32), shape((32, LANES), f32), shape((16, LANES), f32)),
            in_specs=[vmem] * 7,
            out_specs=(vmem, vmem, vmem),
            scratch_shapes=[
                big(600),
                big(40),
                big(32),
                big(32),
                big(32),
                big(32),
                big(2),
                big(8),
                big(8),
                big(2),
                big(8),
                big(8),
                big(32),
                big(32),
                big(3 * events, chunk),
                big(3 * events - 1, chunk),
                big(events, chunk),
                pltpu.SemaphoreType.DMA((3,)),
                pltpu.SemaphoreType.DMA((3,)),
                pltpu.SemaphoreType.DMA,
                pltpu.SemaphoreType.DMA,
                pltpu.SemaphoreType.DMA,
                pltpu.SemaphoreType.DMA,
            ],
            compiler_params=pltpu.CompilerParams(
                collective_id=0, has_side_effects=True, vmem_limit_bytes=40 << 20
            ),
        )(u, v, mass, lhs, base, jnp.asarray(lane_tables()), jnp.asarray(band_table(events)))
        def apart(x):
            x = x.reshape(4, 2, 4, LANES)[:, :, :, :PYZ].transpose(1, 2, 0, 3)
            return x[0].reshape(1, NPTS), x[1].reshape(1, NPTS)

        (fd, ad), (fv, av) = apart(un), apart(vn)
        return fd, fv, ad, av, sk[:, :PYZ]

    return run


def solution(mesh):
    both = P("event", "cuts")
    return jax.shard_map(
        on_device(mesh.shape["event"], mesh.shape["cuts"]),
        mesh=mesh,
        in_specs=(
            both,
            both,
            both,
            both,
            P("cuts"),
            P(None, "cuts"),
            P(None, "cuts"),
            P("cuts", None),
            P("cuts"),
        ),
        out_specs=(both, both, both, both, P("cuts", None)),
        check_vma=False,
    )
```

time: 437 us -> 43 us (0.10)
  the two profiles are of different devices: /device:TPU:1 before, /device:TPU:2 now
where the time goes in v1:
time: 43 us; the launch traced here: 42.6 us
  Pallas kernels  27.1 us (63%)
  local copies, waits for them, and re-layouts  10.5 us (24%)
  other arithmetic  3.26 us (8%)
  between operations  1.68 us (4%)
    pallas_call x1, Pallas kernels, run(): pl.pallas_call(functools.partial(step_kernel, events, slices), out_shape=...  27.1 us
    unnamed x17, local copies, waits for them, and re-layouts  5.48 us
    another operation x4, local copies, waits for them, and re-layouts, apart(): return (x[0].reshape(1, NPTS), x[1].reshape(1, NPTS))  3.22 us
    unnamed x4, other arithmetic  1.58 us

profile of v1, /device:TPU:2, one launch (start us, length us, event | category | flops | bytes accessed | tf_op | source)
XLA Modules:
  0.0 42.6 jit_solution(5912981794345563621)
XLA Ops:
  0.6 1.1 %reduce.2 = f32[17424]{0:T(1024)S(1)} reduce(f32[1,17424]{1,0:T(1,128)} %param.13, f32[]{:T(128)} %constant.42), dimensions={0}, to_apply=%param.13.reduce_sub_computation | reduce | bytes 139396 | tf_op args[1]
  1.7 0.1 reshape_squeeze.26
  1.9 0.8 %copy-done.4 = f32[1,17424]{1,0:T(1,128)S(1)} copy-done((f32[1,17424]{1,0:T(1,128)S(1)}, f32[1,17424]{1,0:T(1,128)}, u32[]{:S(2)}) %copy-start.4) | copy-done | bytes 69720
  2.7 0.2 reduce.3
  2.9 0.1 reshape_squeeze.27
  3.1 0.1 reshape.125.v_ref
  3.2 0.8 %copy-done.5 = f32[1,17424]{1,0:T(1,128)S(1)} copy-done((f32[1,17424]{1,0:T(1,128)S(1)}, f32[1,17424]{1,0:T(1,128)}, u32[]{:S(2)}) %copy-start.5) | copy-done | bytes 69720
  4.0 0.2 reduce
  4.2 0.1 reshape_squeeze.24
  4.3 0.8 %copy-done.6 = f32[1,17424]{1,0:T(1,128)S(1)} copy-done((f32[1,17424]{1,0:T(1,128)S(1)}, f32[1,17424]{1,0:T(1,128)}, u32[]{:S(2)}) %copy-start.6) | copy-done | bytes 69720
  5.2 0.2 reduce.1
  5.3 0.1 reshape_squeeze.25
  5.6 0.1 reshape.124.u_ref
  5.6 0.7 %slice_bitcast_fusion.2 = (s32[256,1]{0,1:T(1,128)S(1)}, s32[1,256]{1,0:T(1,128)S(1)}) fusion(s32[125,256]{1,0:T(8,128)} %param.18), kind=kLoop, calls=%fused_computation.18 | loop fusion | flops 2048 | bytes 3072 | tf_op jit(solution)/shard_map/squeeze | solution.py:376
  7.1 0.6 %copy-done.7 = f32[125]{0:T(128)S(1)} copy-done((f32[125]{0:T(128)S(1)}, f32[125]{0:T(128)}, u32[]{:S(2)}) %copy-start.7) | copy-done | bytes 524
  7.7 0.1 multiply_multiply_fusion
  7.8 0.1 copy.44
  7.9 0.1 mul.51
  8.0 0.2 mul.52
  8.3 0.1 copy.45
  8.4 0.7 %fusion.1 = s32[256,1]{0,1:T(1,128)S(1)} fusion(s32[125,256]{1,0:T(8,128)} %param.18), kind=kLoop, calls=%fused_computation.17 | loop fusion | flops 2304 | bytes 2048 | tf_op jit(solution)/shard_map/mul | solution.py:378
  9.2 0.1 copy.46
  9.3 0.9 %copy-done.3 = f32[17424]{0:T(1024)S(1)} copy-done((f32[17424]{0:T(1024)S(1)}, f32[17424]{0:T(1024)}, u32[]{:S(2)}) %copy-start.3) | copy-done | bytes 69720
  10.2 0.1 reshape.126
  10.4 0.1 reshape.127.mass_ref
  10.5 0.8 %copy-done = f32[56,1152]{1,0:T(8,128)S(1)} copy-done((f32[56,1152]{1,0:T(8,128)S(1)}, f32[56,1152]{1,0:T(8,128)}, u32[]{:S(2)}) %copy-start) | copy-done | bytes 258072
  11.3 27.1 %shard_map.146 = (f32[32,1152]{1,0:T(8,128)S(1)}, f32[32,1152]{1,0:T(8,128)S(1)}, f32[16,1152]{1,0:T(8,128)S(1)}) custom-call(f32[32,1152]{1,0:T(8,128)S(1)} %reshape.124.u_ref, f32[32,1152]{1,0:T(8,128)S(1)} %reshape.125.v_ref, f32[32,1152]{1,0:T(8,128)S(1)} %reshape.127.mass_ref, f32[600,256]{1,0:T(8,128)S(1)} %bitcast.30, s32[256,1]{1,0:T(8,128)S(1)} %sub.20.base_ref, ...), custom_call_target="tpu_custom_call" | custom-call | tf_op jit(solution)/shard_map/pallas_call | solution.py:389
  38.5 0.8 %reshape_squeeze.28 = f32[1,17424]{1,0:T(1,128)} reshape(f32[1,4,4,1089]{3,2,1,0:T(4,128)S(1)} %copy.47) | data formatting | bytes 139392 | tf_op jit(solution)/shard_map/reshape;squeeze | solution.py:425
  39.5 0.8 %reshape_squeeze.29 = f32[1,17424]{1,0:T(1,128)} reshape(f32[1,4,4,1089]{3,2,1,0:T(4,128)S(1)} %copy.48) | data formatting | bytes 139392 | tf_op jit(solution)/shard_map/reshape;squeeze | solution.py:425
  40.3 0.8 %reshape_squeeze.30 = f32[1,17424]{1,0:T(1,128)} reshape(f32[1,4,4,1089]{3,2,1,0:T(4,128)S(1)} %copy.49) | data formatting | bytes 139392 | tf_op jit(solution)/shard_map/reshape;squeeze | solution.py:425
  41.1 0.8 %reshape_squeeze.31 = f32[1,17424]{1,0:T(1,128)} reshape(f32[1,4,4,1089]{3,2,1,0:T(4,128)S(1)} %copy.50) | data formatting | bytes 139392 | tf_op jit(solution)/shard_map/reshape;squeeze | solution.py:425
  41.9 0.6 %copy.53 = f32[16,1089]{1,0:T(8,128)} copy(f32[16,1089]{1,0:T(8,128)S(1)} %bitcast.31) | data formatting | bytes 139392
  (39 shorter events, 0.7 us)
Async XLA Ops:
  1.8 0.9 %copy-start.4 = (f32[1,17424]{1,0:T(1,128)S(1)}, f32[1,17424]{1,0:T(1,128)}, u32[]{:S(2)}) copy-start(f32[1,17424]{1,0:T(1,128)} %param.15) | copy-start | bytes 209092
  3.1 0.9 %copy-start.5 = (f32[1,17424]{1,0:T(1,128)S(1)}, f32[1,17424]{1,0:T(1,128)}, u32[]{:S(2)}) copy-start(f32[1,17424]{1,0:T(1,128)} %param.12) | copy-start | bytes 209092
  4.3 0.9 %copy-start.6 = (f32[1,17424]{1,0:T(1,128)S(1)}, f32[1,17424]{1,0:T(1,128)}, u32[]{:S(2)}) copy-start(f32[1,17424]{1,0:T(1,128)} %param.14) | copy-start | bytes 209092
  5.6 1.5 %copy-start.2 = (f32[125,256]{1,0:T(8,128)S(1)}, f32[125,256]{1,0:T(8,128)}, u32[]{:S(2)}) copy-start(f32[125,256]{1,0:T(8,128)} %param.17) | copy-start | bytes 384004
  7.0 0.7 %copy-start.7 = (f32[125]{0:T(128)S(1)}, f32[125]{0:T(128)}, u32[]{:S(2)}) copy-start(f32[125]{0:T(128)} %constant.21.clone) | copy-start | bytes 1504
  9.3 0.9 %copy-start.3 = (f32[17424]{0:T(1024)S(1)}, f32[17424]{0:T(1024)}, u32[]{:S(2)}) copy-start(f32[17424]{0:T(1024)} %param.16) | copy-start | bytes 209092
  10.4 1.0 %copy-start = (f32[56,1152]{1,0:T(8,128)S(1)}, f32[56,1152]{1,0:T(8,128)}, u32[]{:S(2)}) copy-start(f32[56,1152]{1,0:T(8,128)} %constant.22.clone.coef_ref) | copy-start | bytes 774148
  10.4 0.9 %copy-start.1 = (f32[48,32]{1,0:T(8,128)S(1)}, f32[48,32]{1,0:T(8,128)}, u32[]{:S(2)}) copy-start(f32[48,32]{1,0:T(8,128)} %constant.23.clone.band_ref) | copy-start | bytes 18436

commit v2 on v1

--- a/solution.py
+++ b/solution.py
@@ -66,20 +66,14 @@
     return np.pad(rows, ((0, 56 - rows.shape[0]), (0, 0)))
 
 
-def band_table(events):
+def band_table():
     sigma = PXU / 4.0
     w = lambda d: np.exp(-d * d / (2.0 * sigma * sigma))
     norm = np.sum(w(np.arange(-PXU, PXU + 1).astype(np.float64)))
-    chunk = PXU // events
-    table = np.zeros((events, 3, chunk, PXU))
-    for e in range(events):
-        for o in range(3):
-            for r in range(chunk):
-                gap = 16 * (o - 1) + chunk * e + r - np.arange(PXU)
-                table[e, o, r] = np.where(np.abs(gap) <= PXU, w(gap.astype(np.float64)) / norm, 0.0)
-    table = table.reshape(events * 3 * chunk, 4, 4).transpose(0, 2, 1)
-    table = np.stack([table, np.zeros_like(table)], axis=2)
-    return table.reshape(events * 3 * chunk, 2 * PXU).astype(np.float32)
+    gap = np.arange(-PXU, 2 * PXU)[None, :] - np.arange(PXU)[:, None]
+    table = np.where(np.abs(gap) <= PXU, w(gap.astype(np.float64)) / norm, 0.0)
+    table = table.reshape(PXU, 3, 4, 4).transpose(0, 1, 3, 2).reshape(PXU, 48)
+    return np.pad(-table, ((0, 0), (0, 80))).astype(np.float32)
 
 
 def shifted(x, step):
@@ -116,19 +110,98 @@
     return total
 
 
+FIRST = [PYZ * i // 128 for i in range(4)]
+LEAD = [PYZ * i % 128 for i in range(4)]
+GROUP = 34
+
+
+def lane_starts(i, lane_row):
+    return LEAD[i] + 4 * (lane_row % 4)
+
+
+def run_of(flat_ref, start, size):
+    if len(flat_ref.shape) == 1:
+        return flat_ref[start : start + size]
+    return flat_ref[0:1, start : start + size]
+
+
+def flat_to_rows(flat_ref, both, first):
+    for g in range(17):
+        both[first + 8 * g : first + 8 * g + 8, :] = run_of(flat_ref, 1024 * g, 1024).reshape(8, 128)
+
+
+def planes(both, tail_row, i, lane, row):
+    tiles = []
+    for t in range(10):
+        at = FIRST[i] + t
+        tile = both[pl.ds(at, 8, stride=GROUP), :]
+        if i == 3 and t == 9:
+            tile = jnp.where(row == 3, tail_row, tile)
+        if LEAD[i]:
+            tile = pltpu.roll(tile, 128 - LEAD[i], 1)
+        tile = jnp.where(row % 2 == 1, pltpu.roll(tile, 124, 1), tile)
+        tiles.append(jnp.where(row % 4 >= 2, pltpu.roll(tile, 120, 1), tile))
+    keep = lane < 128 - lane_starts(i, row)
+    return jnp.concatenate([jnp.where(keep, tiles[t], tiles[t + 1]) for t in range(9)], axis=1)
+
+
+def planes_to_flat(slabs, out_refs, rows_refs, lane, row):
+    before = None
+    done = []
+    for i in range(4):
+        tiles = []
+        for t in range(9):
+            tile = slabs[i][:, 128 * t : 128 * t + 128]
+            if LEAD[i]:
+                tile = pltpu.roll(tile, LEAD[i], 1)
+            tile = jnp.where(row % 2 == 1, pltpu.roll(tile, 4, 1), tile)
+            tiles.append(jnp.where(row % 4 >= 2, pltpu.roll(tile, 8, 1), tile))
+        start = lane < lane_starts(i, row)
+        count = (FIRST + [GROUP])[i + 1] - FIRST[i]
+        for t in range(count):
+            low = tiles[t - 1] if t else before
+            done.append(tiles[t] if low is None else jnp.where(start, low, tiles[t]))
+        before = tiles[8] if count == 9 else jnp.where(start, tiles[7], tiles[8])
+    done[0] = jnp.where(lane < lane_starts(0, row), pltpu.roll(before, 1, 0), done[0])
+    for f in range(2):
+        rows = rows_refs[f]
+        for g in range(GROUP):
+            rows[pl.ds(g, 4, stride=GROUP), :] = done[g][4 * f : 4 * f + 4, :]
+        for g in range(17):
+            out_refs[f][0:1, 1024 * g : 1024 * g + 1024] = rows[8 * g : 8 * g + 8, :].reshape(1, 1024)
+        out_refs[f][0:1, 17408:17424] = before[4 * f + 3 : 4 * f + 4, 0:16]
+
+
 def step_kernel(
     events,
     slices,
-    u_ref,
-    v_ref,
-    mass_ref,
-    lhs_ref,
-    base_ref,
+    fd_hbm,
+    fv_hbm,
+    ad_hbm,
+    av_hbm,
+    mass_hbm,
+    shear_hbm,
+    conn_hbm,
+    count_ref,
+    coef_hbm,
+    band_hbm,
+    fdn_ref,
+    fvn_ref,
+    adn_ref,
+    avn_ref,
+    sk_ref,
+    flats,
+    mass_flat,
+    both,
+    tails,
+    rows_a,
+    rows_b,
+    shear_ref,
+    conn_ref,
     coef_ref,
     band_ref,
-    un_ref,
-    vn_ref,
-    sk_ref,
+    u_ref,
+    lhs,
     placed,
     ax,
     aym,
@@ -145,55 +218,77 @@
     kern,
     part,
     recv,
-    rows,
+    total_ref,
+    halo,
+    cols,
+    load_sem,
     halo_send,
     halo_recv,
     part_send,
     part_recv,
-    rows_send,
-    rows_recv,
+    edge_send,
+    edge_recv,
+    cols_send,
+    cols_recv,
 ):
-    chunk = PXU // events
-    others = 3 * events - 1
+    f32 = jnp.float32
     e = lax.axis_index("event")
     s = lax.axis_index("cuts")
     ahead, behind = lax.rem(s + 1, slices), lax.rem(s + slices - 1, slices)
 
-    def partner(m):
-        step = lax.rem(m + 1, 3)
-        return {
-            "event": lax.rem(e + (m + 1) // 3, events),
-            "cuts": lax.rem(s + step + jnp.where(step == 2, slices - 3, 0), slices),
-        }
-
     barrier = pltpu.get_barrier_semaphore()
-
-    def greet(m, carry):
-        pl.semaphore_signal(barrier, inc=1, device_id=partner(m), device_id_type=MESH)
-        return carry
-
-    lax.fori_loop(0, others, greet, 0)
-
+    for to in (ahead, behind):
+        pl.semaphore_signal(barrier, inc=1, device_id={"cuts": to}, device_id_type=MESH)
+
+    def event_at(m):
+        return {"event": lax.rem(e + m, events)}
+
+    for m in range(1, events):
+        pl.semaphore_signal(barrier, inc=1, device_id=event_at(m), device_id_type=MESH)
+
+    loads = [
+        pltpu.make_async_copy(src, dst, load_sem.at[n])
+        for n, (src, dst) in enumerate(
+            (
+                (fd_hbm, flats.at[0]),
+                (ad_hbm, flats.at[1]),
+                (conn_hbm.at[pl.ds(0, 8), :], conn_ref),
+                (shear_hbm, shear_ref),
+                (coef_hbm, coef_ref),
+                (fv_hbm, flats.at[2]),
+                (av_hbm, flats.at[3]),
+                (mass_hbm, mass_flat),
+                (band_hbm, band_ref),
+            )
+        )
+    ]
+    for load in loads:
+        load.start()
+
+    row = lax.broadcasted_iota(jnp.int32, (8, LANES), 0)
+    row1 = lax.broadcasted_iota(jnp.int32, (8, 128), 0)
+    lane1 = lax.broadcasted_iota(jnp.int32, (8, 128), 1)
+
+    def slabs_of(first, second):
+        flat_to_rows(first, both, 0)
+        flat_to_rows(second, both, 136)
+        tails[...] = jnp.zeros((8, 128), f32)
+        tails[0:1, 0:16] = run_of(first, 17408, 16).reshape(1, 16)
+        both[272:280, :] = jnp.zeros((8, 128), f32)
+        both[272:273, 0:16] = run_of(second, 17408, 16).reshape(1, 16)
+        return [planes(both, tails[0:1, :], i, lane1, row1) for i in range(4)]
+
+    loads[0].wait()
+    loads[1].wait()
+    for i, value in enumerate(slabs_of(flats.at[0], flats.at[1])):
+        u_ref[8 * i : 8 * i + 8, :] = value
     for f in range(2):
         stage_g[f : f + 1, :] = u_ref[4 * f : 4 * f + 1, :]
         for i in range(4):
             at = 8 * i + 4 * f + 3
             stage_u[2 * i + f : 2 * i + f + 1, :] = u_ref[at : at + 1, :]
 
-    lhs = lhs_ref[...]
-    hi = lhs.astype(jnp.bfloat16)
-    rest = lhs - hi.astype(jnp.float32)
-    mid = rest.astype(jnp.bfloat16)
-    low = (rest - mid.astype(jnp.float32)).astype(jnp.bfloat16)
-    lane = lax.broadcasted_iota(jnp.int32, (256, LANES), 1)
-    pick = jnp.where(base_ref[...] == lane, 1.0, 0.0).astype(jnp.bfloat16)
-    placed[...] = (
-        jnp.dot(hi, pick, preferred_element_type=jnp.float32)
-        + jnp.dot(mid, pick, preferred_element_type=jnp.float32)
-        + jnp.dot(low, pick, preferred_element_type=jnp.float32)
-    )
-
-    pl.semaphore_wait(barrier, others)
+    pl.semaphore_wait(barrier, events + 1)
     to_behind = pltpu.make_async_remote_copy(
         stage_g, ghost, halo_send.at[0], halo_recv.at[0], {"cuts": behind}, MESH
     )
@@ -203,15 +298,55 @@
     )
     to_ahead.start()
 
+    for n in (2, 3):
+        loads[n].wait()
+    first = conn_ref[0:1, :]
+    layer = sum(jnp.where(first >= 4 * PYZ * n, 1, 0) for n in (1, 2, 3))
+    base = jnp.broadcast_to(first - 4 * PYZ * layer, (128, 256)).T
+    wide_row = lax.broadcasted_iota(jnp.int32, (8, 256), 0)
+    slot = lax.broadcasted_iota(jnp.int32, (8, 256), 1)
+    own = jnp.where((wide_row % 4 == layer) & (slot < count_ref[0]), 1.0, 0.0)
+
+    def flux_rows(c, jk):
+        if jk == 25:
+            return jnp.zeros((8, 256), f32)
+        near = 50 * c + jk
+        value = float(CUBE[near]) * shear_ref[near : near + 1, :]
+        if c < 2:
+            far = near + 25
+            value = jnp.where(wide_row < 4, value, float(CUBE[far]) * shear_ref[far : far + 1, :])
+        else:
+            value = jnp.where(wide_row < 4, value, 0.0)
+        return value * own
+
+    for c in range(3):
+        for pair in range(13):
+            value = jnp.concatenate([flux_rows(c, 2 * pair), flux_rows(c, 2 * pair + 1)], axis=0)
+            at = 208 * c + 16 * pair
+            hi = value.astype(jnp.bfloat16)
+            rest = value - hi.astype(f32)
+            mid = rest.astype(jnp.bfloat16)
+            lhs[0, at : at + 16, :] = hi
+            lhs[1, at : at + 16, :] = mid
+            lhs[2, at : at + 16, :] = (rest - mid.astype(f32)).astype(jnp.bfloat16)
+    lane_wide = lax.broadcasted_iota(jnp.int32, (256, 128), 1)
+    pick = jnp.concatenate(
+        [jnp.where(base == lane_wide + 128 * t, 1.0, 0.0).astype(jnp.bfloat16) for t in range(9)], axis=1
+    )
+    placed[...] = (
+        jnp.dot(lhs[0], pick, preferred_element_type=f32)
+        + jnp.dot(lhs[1], pick, preferred_element_type=f32)
+        + jnp.dot(lhs[2], pick, preferred_element_type=f32)
+    )
+
     twice = lambda x: jnp.concatenate([x, x], axis=0)
-    row = lax.broadcasted_iota(jnp.int32, (8, LANES), 0)
     kinds = (aym, aye, azm, aze)
     for c in (2, 0, 1):
         sums = [None] * 4
         for j in range(5):
             for k in range(5):
-                first = 24 * (5 * j + k) + 8 * c
-                moved = shifted(placed[first : first + 8, :], -(PZ * j + k))
+                at = 208 * c + 8 * (5 * j + k)
+                moved = shifted(placed[at : at + 8, :], -(PZ * j + k))
                 q = 2 * (j == 4) + (k == 4)
                 sums[q] = moved if sums[q] is None else sums[q] + moved
         mm, me, em, ee = sums
@@ -240,6 +375,7 @@
     )
     flux_ahead.start()
 
+    loads[4].wait()
     for i in (1, 2, 3, 0):
         at = 8 * i
         if i == 0:
@@ -308,37 +444,61 @@
         kern[8 * i : 8 * i + 8, :] += prods[i]
         force[8 * i : 8 * i + 8, :] += turned[i]
 
-    added = jnp.dot(
-        -band_ref[...],
-        kern[...],
+    for half in range(2):
+        both_nodes = jnp.where(
+            row < 4, kern[16 * half : 16 * half + 8, :], kern[16 * half + 8 : 16 * half + 16, :]
+        )
+        for m in range(events):
+            part[m, 8 * half : 8 * half + 8, :] = both_nodes[:, 128 * m : 128 * m + 128]
+            part[m, 16 + 8 * half : 24 + 8 * half, :] = both_nodes[:, 128 * events : LANES]
+    for m in range(1, events):
+        to = event_at(m)
+        pltpu.make_async_remote_copy(
+            part.at[to["event"]], recv.at[m - 1], part_send, part_recv, to, MESH
+        ).start()
+
+    for n in (5, 6, 7, 8):
+        loads[n].wait()
+    mass = slabs_of(mass_flat, mass_flat)
+    sign = jnp.where(row < 4, time_step, -time_step)
+    speeds = [
+        speed + (sign * mass[i]) * force[8 * i : 8 * i + 8, :] for i, speed in enumerate(slabs_of(flats.at[2], flats.at[3]))
+    ]
+    planes_to_flat(speeds, (fvn_ref, avn_ref), (rows_a, rows_b), lane1, row1)
+    moved = [u_ref[8 * i : 8 * i + 8, :] - sign * speeds[i] for i in range(4)]
+    planes_to_flat(moved, (fdn_ref, adn_ref), (rows_a, rows_b), lane1, row1)
+
+    pltpu.make_async_copy(recv, recv, part_recv).wait()
+    total = part[e]
+    for m in range(events - 1):
+        total = total + recv[m]
+    total_ref[...] = total
+    edges = [
+        pltpu.make_async_remote_copy(
+            total_ref, halo.at[n], edge_send.at[n], edge_recv.at[n], {"cuts": to}, MESH
+        )
+        for n, to in enumerate((ahead, behind))
+    ]
+    for edge in edges:
+        edge.start()
+    for edge in edges:
+        edge.wait()
+    tall = lambda at: jnp.concatenate(
+        [halo[0, at : at + 16, :], total_ref[at : at + 16, :], halo[1, at : at + 16, :]], axis=0
+    )
+    along = jnp.dot(
+        band_ref[:, 0:48],
+        jnp.concatenate([tall(0), tall(16)], axis=1),
         precision=lax.Precision.HIGHEST,
-        preferred_element_type=jnp.float32,
-    )
-    for m in range(3 * events):
-        part[m] = added[chunk * m : chunk * m + chunk, :]
-
-    def spray(m, carry):
-        step = lax.rem(m + 1, 3)
-        to = partner(m)
-        slot = 3 * to["event"] + lax.rem(step + 1, 3)
-        pltpu.make_async_remote_copy(
-            part.at[slot], recv.at[m], part_send, part_recv, to, MESH
-        ).start()
-        return carry
-
-    lax.fori_loop(0, others, spray, 0)
-
-    for i in range(4):
-        at = slice(8 * i, 8 * i + 8)
-        step = jnp.where(row < 4, time_step, -time_step)
-        speed = v_ref[at, :] + (step * mass_ref[at, :]) * force[at, :]
-        vn_ref[at, :] = speed
-        un_ref[at, :] = u_ref[at, :] - step * speed
-
-    pltpu.make_async_copy(recv, recv, part_recv).wait()
-    total = part[3 * e + 1]
-    for m in range(others):
-        total = total + recv[m]
+        preferred_element_type=f32,
+    )
+    cols[e] = along[:, 0:128]
+    for m in range(1, events):
+        pltpu.make_async_remote_copy(cols.at[e], cols.at[e], cols_send, cols_recv, event_at(m), MESH).start()
+    pltpu.make_async_copy(recv, recv, part_send).wait()
+    some = cols.at[pl.ds(0, events - 1)]
+    pltpu.make_async_copy(some, some, cols_recv).wait()
+    total = jnp.concatenate([cols[m] for m in range(events)] + [along[:, 128:256]], axis=1)
     across = None
     for d in range(-cross_reach, cross_reach + 1):
         term = coef_ref[20 + d : 21 + d, :] * shifted(total, PZ * d)
@@ -347,52 +507,49 @@
     for d in range(-cross_reach, cross_reach + 1):
         term = coef_ref[29 + d : 30 + d, :] * shifted(total, d)
         across = term if across is None else across + term
-    rows[e] = across
-
-    def share(m, carry):
-        to = {"event": lax.rem(e + m + 1, events)}
-        pltpu.make_async_remote_copy(
-            rows.at[e], rows.at[e], rows_send, rows_recv, to, MESH
-        ).start()
-        return carry
-
-    lax.fori_loop(0, events - 1, share, 0)
-    pltpu.make_async_copy(recv, recv, part_send).wait()
-    some = rows.at[pl.ds(0, events - 1)]
-    pltpu.make_async_copy(some, some, rows_recv).wait()
-    pltpu.make_async_copy(some, some, rows_send).wait()
-    for m in range(events):
-        sk_ref[chunk * m : chunk * m + chunk, :] = rows[m]
+    sk_ref[...] = across[:, 0:PYZ]
+    pltpu.make_async_copy(some, some, cols_send).wait()
+
+
+def store_kernel(a, b, c, d, k, a_hbm, b_hbm, c_hbm, d_hbm, k_hbm, sem):
+    pairs = ((k, k_hbm), (a, a_hbm), (b, b_hbm), (c, c_hbm), (d, d_hbm))
+    copies = [pltpu.make_async_copy(src, dst, sem.at[n]) for n, (src, dst) in enumerate(pairs)]
+    for copy in copies:
+        copy.start()
+    for copy in copies:
+        copy.wait()
 
 
 def on_device(events, slices):
     def run(fd, fv, ad, av, inverse_mass, shear, connectivity, face_points, count):
-        chunk = PXU // events
-        layers = lambda x: jnp.pad(x.reshape(4, 4, PYZ), ((0, 0), (0, 0), (0, LANES - PYZ)))
-        pair = lambda x, y: jnp.stack([layers(x), layers(y)]).transpose(2, 0, 1, 3).reshape(32, LANES)
-        u = pair(fd[0], ad[0])
-        v = pair(fv[0], av[0])
-        mass = pair(inverse_mass, inverse_mass)
-        first = connectivity[0]
-        layer = first // (4 * PYZ)
-        base = (first - 4 * PYZ * layer).reshape(256, 1)
-        active = (jnp.arange(256, dtype=jnp.int32) < count[0]).astype(jnp.float32)
-        flux = jnp.asarray(CUBE)[:, None] * shear * active[None, :]
-        own = (layer[None, :] == jnp.arange(4, dtype=jnp.int32)[:, None]).astype(jnp.float32)
-        cube = flux.reshape(5, 25, 256).transpose(1, 0, 2)
-        lhs = (cube[:, :, None, :] * own[None, None, :, :]).reshape(25, 20, 256)
-        lhs = jnp.pad(lhs, ((0, 0), (0, 4), (0, 0))).reshape(600, 256)
         vmem = pl.BlockSpec(memory_space=pltpu.VMEM)
-        shape = jax.ShapeDtypeStruct
+        there = pl.BlockSpec(memory_space=pltpu.HBM)
+        stay = lambda x: pltpu.with_memory_space_constraint(x, pltpu.HBM)
         f32 = jnp.float32
+        flat = jax.ShapeDtypeStruct((1, NPTS), f32)
+        table = jax.ShapeDtypeStruct((PXU, PYZ), f32)
         big = lambda *dims: pltpu.VMEM((*dims, LANES), f32)
-        un, vn, sk = pl.pallas_call(
+        small = lambda *dims: pltpu.VMEM((*dims, 128), f32)
+        dma = pltpu.SemaphoreType.DMA
+        outs = pl.pallas_call(
             functools.partial(step_kernel, events, slices),
-            out_shape=(shape((32, LANES), f32), shape((32, LANES), f32), shape((16, LANES), f32)),
-            in_specs=[vmem] * 7,
-            out_specs=(vmem, vmem, vmem),
+            out_shape=(flat, flat, flat, flat, table),
+            in_specs=[there] * 7 + [pl.BlockSpec(memory_space=pltpu.SMEM)] + [there] * 2,
+            out_specs=(vmem,) * 5,
             scratch_shapes=[
-                big(600),
+                pltpu.VMEM((4, 1, NPTS), f32),
+                pltpu.VMEM((NPTS,), f32),
+                small(280),
+                small(8),
+                small(136),
+                small(136),
+                pltpu.VMEM((125, 256), f32),
+                pltpu.VMEM((8, 256), jnp.int32),
+                big(56),
+                small(16),
+                big(32),
+                pltpu.VMEM((3, 624, 256), jnp.bfloat16),
+                big(624),
                 big(40),
                 big(32),
                 big(32),
@@ -406,26 +563,39 @@
                 big(8),
                 big(32),
                 big(32),
-                big(3 * events, chunk),
-                big(3 * events - 1, chunk),
-                big(events, chunk),
-                pltpu.SemaphoreType.DMA((3,)),
-                pltpu.SemaphoreType.DMA((3,)),
-                pltpu.SemaphoreType.DMA,
-                pltpu.SemaphoreType.DMA,
-                pltpu.SemaphoreType.DMA,
-                pltpu.SemaphoreType.DMA,
+                small(events, 32),
+                small(events - 1, 32),
+                small(32),
+                small(2, 32),
+                small(events, 16),
+                dma((9,)),
+                dma((3,)),
+                dma((3,)),
+                dma,
+                dma,
+                dma((2,)),
+                dma((2,)),
+                dma,
+                dma,
             ],
             compiler_params=pltpu.CompilerParams(
                 collective_id=0, has_side_effects=True, vmem_limit_bytes=40 << 20
             ),
-        )(u, v, mass, lhs, base, jnp.asarray(lane_tables()), jnp.asarray(band_table(events)))
-        def apart(x):
-            x = x.reshape(4, 2, 4, LANES)[:, :, :, :PYZ].transpose(1, 2, 0, 3)
-            return x[0].reshape(1, NPTS), x[1].reshape(1, NPTS)
-
-        (fd, ad), (fv, av) = apart(un), apart(vn)
-        return fd, fv, ad, av, sk[:, :PYZ]
+        )(
+            *map(stay, (fd, fv, ad, av, inverse_mass, shear, connectivity)),
+            count,
+            stay(jnp.asarray(lane_tables())),
+            stay(jnp.asarray(band_table())),
+        )
+        fdn, fvn, adn, avn, sk = pl.pallas_call(
+            store_kernel,
+            out_shape=(flat, flat, flat, flat, table),
+            in_specs=[vmem] * 5,
+            out_specs=(there,) * 5,
+            scratch_shapes=[dma((5,))],
+            compiler_params=pltpu.CompilerParams(vmem_limit_bytes=4 << 20),
+        )(*outs)
+        return fdn, fvn, adn, avn, sk
 
     return run
 

time: 43 us -> 28.4 us (0.66)
  the two profiles are of different devices: /device:TPU:2 before, /device:TPU:1 now
where the time goes in v2:
time: 28.4 us; the launch traced here: 28.3 us
  Pallas kernels  27 us (95%)
  between operations  1.29 us (5%)
    pallas_call x1, Pallas kernels, run(): pl.pallas_call(functools.partial(step_kernel, events, slices), out_shape=...  26.3 us
    pallas_call x1, Pallas kernels, run(): pl.pallas_call(store_kernel, out_shape=(flat, flat, flat, flat, table), i...  0.77 us

profile of v2, /device:TPU:1, one launch (start us, length us, event | category | flops | bytes accessed | tf_op | source)
XLA Modules:
  0.0 28.3 jit_solution(8449166137984462008)
XLA Ops:
  1.3 26.3 %shard_map.137 = (f32[1,17424]{1,0:T(1,128)S(1)}, f32[1,17424]{1,0:T(1,128)S(1)}, f32[1,17424]{1,0:T(1,128)S(1)}, f32[1,17424]{1,0:T(1,128)S(1)}, f32[16,1089]{1,0:T(8,128)S(1)}) custom-call(f32[1,17424]{1,0:T(1,128)} %fd_hbm.1, f32[1,17424]{1,0:T(1,128)} %fv_hbm.1, f32[1,17424]{1,0:T(1,128)} %ad_hbm.1, f32[1,17424]{1,0:T(1,128)} %av_hbm.1, f32[17424]{0:T(1024)} %mass_hbm.1, ...), custom_call_target="tpu_custom_call" | custom-call | tf_op jit(solution)/shard_map/pallas_call | solution.py:534
  27.5 0.8 %shard_map.138 = (f32[1,17424]{1,0:T(1,128)}, f32[1,17424]{1,0:T(1,128)}, f32[1,17424]{1,0:T(1,128)}, f32[1,17424]{1,0:T(1,128)}, f32[16,1089]{1,0:T(8,128)}) custom-call(f32[1,17424]{1,0:T(1,128)S(1)} %get-tuple-element.10.a, f32[1,17424]{1,0:T(1,128)S(1)} %get-tuple-element.11.b, f32[1,17424]{1,0:T(1,128)S(1)} %get-tuple-element.12.c, ...), custom_call_target="tpu_custom_call" | custom-call | tf_op jit(solution)/shard_map/pallas_call | solution.py:590

commit v3 on v2

--- a/solution.py
+++ b/solution.py
@@ -70,10 +70,16 @@
     sigma = PXU / 4.0
     w = lambda d: np.exp(-d * d / (2.0 * sigma * sigma))
     norm = np.sum(w(np.arange(-PXU, PXU + 1).astype(np.float64)))
-    gap = np.arange(-PXU, 2 * PXU)[None, :] - np.arange(PXU)[:, None]
-    table = np.where(np.abs(gap) <= PXU, w(gap.astype(np.float64)) / norm, 0.0)
-    table = table.reshape(PXU, 3, 4, 4).transpose(0, 1, 3, 2).reshape(PXU, 48)
-    return np.pad(-table, ((0, 0), (0, 80))).astype(np.float32)
+
+    def table(places):
+        gap = places[None, :] - np.arange(PXU)[:, None]
+        return np.where(np.abs(gap) <= PXU, w(gap.astype(np.float64)) / norm, 0.0)
+
+    rows = table(np.arange(-PXU, 2 * PXU)).reshape(PXU, 3, 4, 4).transpose(0, 1, 3, 2).reshape(PXU, 48)
+    places = PXU * np.arange(-2, 3)[:, None] + np.array([-4, -3, -2, -1, 16])[None, :]
+    extra = np.pad(table(places.reshape(25)).reshape(PXU, 5, 5), ((0, 0), (0, 0), (0, 3)))
+    both = np.concatenate([rows, extra.reshape(PXU, 40)], axis=1)
+    return np.pad(-both, ((0, 0), (0, 40))).astype(np.float32)
 
 
 def shifted(x, step):
@@ -145,7 +151,7 @@
     return jnp.concatenate([jnp.where(keep, tiles[t], tiles[t + 1]) for t in range(9)], axis=1)
 
 
-def planes_to_flat(slabs, out_refs, rows_refs, lane, row):
+def planes_to_flat(slabs, rows_refs, lane, row):
     before = None
     done = []
     for i in range(4):
@@ -167,9 +173,7 @@
         rows = rows_refs[f]
         for g in range(GROUP):
             rows[pl.ds(g, 4, stride=GROUP), :] = done[g][4 * f : 4 * f + 4, :]
-        for g in range(17):
-            out_refs[f][0:1, 1024 * g : 1024 * g + 1024] = rows[8 * g : 8 * g + 8, :].reshape(1, 1024)
-        out_refs[f][0:1, 17408:17424] = before[4 * f + 3 : 4 * f + 4, 0:16]
+    return [before[4 * f + 3 : 4 * f + 4, 0:16] for f in range(2)]
 
 
 def step_kernel(
@@ -208,37 +212,49 @@
     aye,
     azm,
     aze,
+    carried,
+    returned,
     ghost,
     tail_u,
     tail_a,
     stage_g,
+    stage_f,
+    stage_r,
     stage_u,
     stage_a,
     force,
     kern,
     part,
     recv,
+    recv_short,
     total_ref,
     halo,
+    halo_far,
     cols,
+    lone,
     load_sem,
     halo_send,
     halo_recv,
     part_send,
     part_recv,
+    short_send,
+    short_recv,
     edge_send,
     edge_recv,
     cols_send,
     cols_recv,
+    lone_send,
+    lone_recv,
 ):
     f32 = jnp.float32
     e = lax.axis_index("event")
     s = lax.axis_index("cuts")
-    ahead, behind = lax.rem(s + 1, slices), lax.rem(s + slices - 1, slices)
+    first, final = s == 0, s == slices - 1
+    cut_at = lambda m: {"cuts": lax.rem(s + m + slices, slices)}
 
     barrier = pltpu.get_barrier_semaphore()
-    for to in (ahead, behind):
-        pl.semaphore_signal(barrier, inc=1, device_id={"cuts": to}, device_id_type=MESH)
+    for m in (-1, 1, -2, 2):
+        pl.semaphore_signal(barrier, inc=1, device_id=cut_at(m), device_id_type=MESH)
 
     def event_at(m):
         return {"event": lax.rem(e + m, events)}
@@ -250,10 +266,10 @@
         pltpu.make_async_copy(src, dst, load_sem.at[n])
         for n, (src, dst) in enumerate(
             (
+                (conn_hbm.at[pl.ds(0, 8), :], conn_ref),
+                (shear_hbm, shear_ref),
                 (fd_hbm, flats.at[0]),
                 (ad_hbm, flats.at[1]),
-                (conn_hbm.at[pl.ds(0, 8), :], conn_ref),
-                (shear_hbm, shear_ref),
                 (coef_hbm, coef_ref),
                 (fv_hbm, flats.at[2]),
                 (av_hbm, flats.at[3]),
@@ -278,31 +294,11 @@
         both[272:273, 0:16] = run_of(second, 17408, 16).reshape(1, 16)
         return [planes(both, tails[0:1, :], i, lane1, row1) for i in range(4)]
 
-    loads[0].wait()
-    loads[1].wait()
-    for i, value in enumerate(slabs_of(flats.at[0], flats.at[1])):
-        u_ref[8 * i : 8 * i + 8, :] = value
-    for f in range(2):
-        stage_g[f : f + 1, :] = u_ref[4 * f : 4 * f + 1, :]
-        for i in range(4):
-            at = 8 * i + 4 * f + 3
-            stage_u[2 * i + f : 2 * i + f + 1, :] = u_ref[at : at + 1, :]
-
-    pl.semaphore_wait(barrier, events + 1)
-    to_behind = pltpu.make_async_remote_copy(
-        stage_g, ghost, halo_send.at[0], halo_recv.at[0], {"cuts": behind}, MESH
-    )
-    to_behind.start()
-    to_ahead = pltpu.make_async_remote_copy(
-        stage_u, tail_u, halo_send.at[1], halo_recv.at[1], {"cuts": ahead}, MESH
-    )
-    to_ahead.start()
-
-    for n in (2, 3):
+    for n in (0, 1):
         loads[n].wait()
-    first = conn_ref[0:1, :]
-    layer = sum(jnp.where(first >= 4 * PYZ * n, 1, 0) for n in (1, 2, 3))
-    base = jnp.broadcast_to(first - 4 * PYZ * layer, (128, 256)).T
+    corner = conn_ref[0:1, :]
+    layer = sum(jnp.where(corner >= 4 * PYZ * n, 1, 0) for n in (1, 2, 3))
+    base = jnp.broadcast_to(corner - 4 * PYZ * layer, (128, 256)).T
     wide_row = lax.broadcasted_iota(jnp.int32, (8, 256), 0)
     slot = lax.broadcasted_iota(jnp.int32, (8, 256), 1)
     own = jnp.where((wide_row % 4 == layer) & (slot < count_ref[0]), 1.0, 0.0)
@@ -324,20 +320,35 @@
             value = jnp.concatenate([flux_rows(c, 2 * pair), flux_rows(c, 2 * pair + 1)], axis=0)
             at = 208 * c + 16 * pair
             hi = value.astype(jnp.bfloat16)
-            rest = value - hi.astype(f32)
-            mid = rest.astype(jnp.bfloat16)
             lhs[0, at : at + 16, :] = hi
-            lhs[1, at : at + 16, :] = mid
-            lhs[2, at : at + 16, :] = (rest - mid.astype(f32)).astype(jnp.bfloat16)
+            lhs[1, at : at + 16, :] = (value - hi.astype(f32)).astype(jnp.bfloat16)
     lane_wide = lax.broadcasted_iota(jnp.int32, (256, 128), 1)
     pick = jnp.concatenate(
         [jnp.where(base == lane_wide + 128 * t, 1.0, 0.0).astype(jnp.bfloat16) for t in range(9)], axis=1
     )
-    placed[...] = (
-        jnp.dot(lhs[0], pick, preferred_element_type=f32)
-        + jnp.dot(lhs[1], pick, preferred_element_type=f32)
-        + jnp.dot(lhs[2], pick, preferred_element_type=f32)
-    )
+    placed[...] = jnp.dot(lhs[0], pick, preferred_element_type=f32) + jnp.dot(
+        lhs[1], pick, preferred_element_type=f32
+    )
+
+    loads[2].wait()
+    loads[3].wait()
+    for i, value in enumerate(slabs_of(flats.at[0], flats.at[1])):
+        u_ref[8 * i : 8 * i + 8, :] = value
+    for f in range(2):
+        stage_g[f : f + 1, :] = u_ref[4 * f : 4 * f + 1, :]
+        for i in range(4):
+            at = 8 * i + 4 * f + 3
+            stage_u[2 * i + f : 2 * i + f + 1, :] = u_ref[at : at + 1, :]
+
+    pl.semaphore_wait(barrier, events + 3)
+    to_behind = pltpu.make_async_remote_copy(
+        stage_g, ghost, halo_send.at[0], halo_recv.at[0], cut_at(-1), MESH
+    )
+    planes_ahead = pltpu.make_async_remote_copy(
+        stage_u, tail_u, halo_send.at[1], halo_recv.at[1], cut_at(1), MESH
+    )
+    pl.when(jnp.logical_not(first))(to_behind.start)
+    pl.when(final)(planes_ahead.start)
 
     twice = lambda x: jnp.concatenate([x, x], axis=0)
     kinds = (aym, aye, azm, aze)
@@ -356,8 +367,8 @@
             ax[32:40, :] = twice(whole[0:4, :])
             for q in range(4):
                 stage_a[4 + q : 5 + q, :] = sums[q][3:4, :]
-                shifted_layer = pltpu.roll(twice(pairs[q][0:4, :]), 1, 0)
-                kinds[q][0:8, :] = jnp.where(row % 4 == 0, 0.0, shifted_layer)
+                moved = pltpu.roll(twice(pairs[q][0:4, :]), 1, 0)
+                kinds[q][0:8, :] = jnp.where(row % 4 == 0, 0.0, moved)
         else:
             for half in range(2):
                 i = 2 * c + half
@@ -371,22 +382,17 @@
                     kinds[q][8 * i : 8 * i + 8, :] = value
 
     flux_ahead = pltpu.make_async_remote_copy(
-        stage_a, tail_a, halo_send.at[2], halo_recv.at[2], {"cuts": ahead}, MESH
-    )
-    flux_ahead.start()
+        stage_a, tail_a, halo_send.at[2], halo_recv.at[2], cut_at(1), MESH
+    )
+    pl.when(final)(flux_ahead.start)
 
     loads[4].wait()
-    for i in (1, 2, 3, 0):
+    axes = ((0, PZ, aym, aye), (8, 1, azm, aze))
+    for i in range(4):
         at = 8 * i
-        if i == 0:
-            flux_ahead.wait()
-            mm, me, em, ee = (tail_a[4 + q : 5 + q, :] for q in range(4))
-            for ref, value in zip(kinds, (mm + me, em + ee, mm + em, me + ee)):
-                ref[0:1, :] += value
-                ref[4:5, :] += value
         u = u_ref[at : at + 8, :]
         ksum = tsum = None
-        for base, stride, m_ref, e_ref in ((0, PZ, aym, aye), (8, 1, azm, aze)):
+        for base, stride, m_ref, e_ref in axes:
             gm, ge = stencil(u, coef_ref, base, stride)
             fm, fe = m_ref[at : at + 8, :] * gm, e_ref[at : at + 8, :] * ge
             term = fm * pltpu.roll(gm, 4, 0) + fe * pltpu.roll(ge, 4, 0)
@@ -396,12 +402,8 @@
         kern[at : at + 8, :] = ksum
         force[at : at + 8, :] = tsum
 
-    to_behind.wait()
-    to_ahead.wait()
     slab = [u_ref[8 * i : 8 * i + 8, :] for i in range(4)]
-    last = pltpu.roll(slab[0], 7, 0)
-    last = jnp.where(row == 3, ghost[0:1, :], jnp.where(row == 7, ghost[1:2, :], last))
-    slab.append(last)
+    slab.append(pltpu.roll(slab[0], 7, 0))
     grads = []
     for a in range(5):
         total = None
@@ -411,94 +413,218 @@
         grads.append(total)
     moved = [ax[8 * a : 8 * a + 8, :] * grads[a] for a in range(5)]
     prods = [moved[a] * pltpu.roll(grads[a], 4, 0) for a in range(5)]
+    inner = row % 4 < 3
+    after_first = row % 4 > 0
+    terms = [kern[8 * i : 8 * i + 8, :] + jnp.where(inner, prods[i], 0.0) for i in range(4)]
+    terms[0] = terms[0] + jnp.where(after_first, pltpu.roll(prods[4], 1, 0), 0.0)
+    for half in range(2):
+        nodes = jnp.where(row < 4, terms[2 * half], terms[2 * half + 1])
+        for m in range(events + 1):
+            part[m, 8 * half : 8 * half + 8, :] = nodes[:, 128 * m : 128 * m + 128]
+    for m in range(events + 1):
+        part[m, 16:24, :] = jnp.zeros((8, 128), f32)
     turned = []
     for a in range(5):
         total = None
         for b in range(5):
             term = D[b][a] * moved[b]
             total = term if total is None else total + term
-        turned.append(total)
-    edge = [tail_u[2 * i : 2 * i + 2, :] for i in range(4)] + [stage_g[...]]
-    edge_flux = [tail_a[i : i + 1, :] for i in range(4)]
-    edge_flux.append(
-        (tail_a[4:5, :] + tail_a[5:6, :]) + (tail_a[6:7, :] + tail_a[7:8, :])
-    )
-    edge_force = edge_kern = None
-    for a in range(5):
-        total = None
-        for b in range(5):
-            term = D[a][b] * edge[b]
-            total = term if total is None else total + term
-        term = (D[a][4] * edge_flux[a]) * total
-        edge_force = term if edge_force is None else edge_force + term
-        if a == 4:
-            edge_kern = edge_flux[4] * total[0:1, :] * total[1:2, :]
-
-    back = pltpu.roll(turned[4], 1, 0)
-    back = jnp.where(row == 0, edge_force[0:1, :], jnp.where(row == 4, edge_force[1:2, :], back))
-    turned[0] = turned[0] + back
-    back = pltpu.roll(prods[4], 1, 0)
-    back = jnp.where(row == 0, edge_kern, back)
-    prods[0] = prods[0] + back
+        turned.append(jnp.where(inner, total, 0.0))
+    turned[0] = turned[0] + jnp.where(after_first, pltpu.roll(turned[4], 1, 0), 0.0)
     for i in range(4):
-        kern[8 * i : 8 * i + 8, :] += prods[i]
         force[8 * i : 8 * i + 8, :] += turned[i]
-
-    for half in range(2):
-        both_nodes = jnp.where(
-            row < 4, kern[16 * half : 16 * half + 8, :], kern[16 * half + 8 : 16 * half + 16, :]
-        )
-        for m in range(events):
-            part[m, 8 * half : 8 * half + 8, :] = both_nodes[:, 128 * m : 128 * m + 128]
-            part[m, 16 + 8 * half : 24 + 8 * half, :] = both_nodes[:, 128 * events : LANES]
+    def slopes_of(plane):
+        return [stencil(plane, coef_ref, base, stride) for base, stride, _, _ in axes]
+
+    def last_layer(planes_ref, flux_ref, plane, slopes=None):
+        edge = [planes_ref[2 * i : 2 * i + 2, :] for i in range(4)] + [plane]
+        mm, me, em, ee = (flux_ref[4 + q : 5 + q, :] for q in range(4))
+        edge_flux = [flux_ref[i : i + 1, :] for i in range(4)] + [(mm + me) + (em + ee)]
+        grads = []
+        for a in range(5):
+            total = None
+            for b in range(5):
+                term = D[a][b] * edge[b]
+                total = term if total is None else total + term
+            grads.append(total)
+        moved = [edge_flux[a] * grads[a] for a in range(5)]
+        across = []
+        for (gm, ge), am, ae in zip(slopes or slopes_of(plane), (mm + me, mm + em), (em + ee, me + ee)):
+            across.append((gm, ge, am * gm, ae * ge))
+        return grads, moved, across
+
+    def last_terms(planes_ref, flux_ref, plane, slopes=None):
+        grads, moved, across = last_layer(planes_ref, flux_ref, plane, slopes)
+        terms = [moved[a][0:1, :] * grads[a][1:2, :] for a in range(5)]
+        for gm, ge, fm, fe in across:
+            terms[4] = terms[4] + fm[0:1, :] * gm[1:2, :] + fe[0:1, :] * ge[1:2, :]
+        return terms
+
+    def last_force(planes_ref, flux_ref, plane):
+        _, moved, across = last_layer(planes_ref, flux_ref, plane)
+        turned = []
+        for a in range(5):
+            total = None
+            for b in range(5):
+                term = D[b][a] * moved[b]
+                total = term if total is None else total + term
+            turned.append(total)
+        for (base, stride, _, _), (_, _, fm, fe) in zip(axes, across):
+            turned[4] = turned[4] + spread(fm, fe, coef_ref, base, stride)
+        return turned
+
+    @pl.when(jnp.logical_not(final))
+    def _():
+        to_behind.wait_recv()
+        terms = last_terms(stage_u, stage_a, ghost[...])
+        for m in range(events + 1):
+            lanes = slice(128 * m, 128 * m + 128)
+            for i in range(4):
+                part[m, 4 * i + 3 : 4 * i + 4, :] += terms[i][:, lanes]
+            part[m, 20:21, :] = terms[4][:, lanes]
+
+    @pl.when(first)
+    def _():
+        plane = stage_g[...]
+        slopes = slopes_of(plane)
+        planes_ahead.wait_recv()
+        flux_ahead.wait_recv()
+        terms = last_terms(tail_u, tail_a, plane, slopes)
+        for m in range(events + 1):
+            lanes = slice(128 * m, 128 * m + 128)
+            part[m, 0:1, :] += terms[4][:, lanes]
+            for i in range(4):
+                part[m, 16 + i : 17 + i, :] = terms[i][:, lanes]
+
+    lead = e == events - 1
     for m in range(1, events):
         to = event_at(m)
         pltpu.make_async_remote_copy(
-            part.at[to["event"]], recv.at[m - 1], part_send, part_recv, to, MESH
+            part.at[to["event"]], recv.at[e], part_send, part_recv, to, MESH
         ).start()
-
-    for n in (5, 6, 7, 8):
+    short_part = pltpu.make_async_remote_copy(
+        part.at[events], recv_short.at[e], short_send, short_recv, {"event": events - 1}, MESH
+    )
+    pl.when(jnp.logical_not(lead))(short_part.start)
+    recv[e] = part[e]
+
+    force_ahead = pltpu.make_async_remote_copy(
+        stage_f, carried, halo_send.at[3], halo_recv.at[3], cut_at(1), MESH
+    )
+    force_back = pltpu.make_async_remote_copy(
+        stage_r, returned, halo_send.at[4], halo_recv.at[4], cut_at(-1), MESH
+    )
+
+    @pl.when(jnp.logical_not(final))
+    def _():
+        turned = last_force(stage_u, stage_a, ghost[...])
+        stage_f[...] = turned[4]
+        force_ahead.start()
+        for i in range(4):
+            for f in range(2):
+                at = 8 * i + 4 * f + 3
+                force[at : at + 1, :] += turned[i][f : f + 1, :]
+
+    @pl.when(first)
+    def _():
+        turned = last_force(tail_u, tail_a, stage_g[...])
+        for i in range(4):
+            stage_r[2 * i : 2 * i + 2, :] = turned[i]
+        force_back.start()
+        for f in range(2):
+            force[4 * f : 4 * f + 1, :] += turned[4][f : f + 1, :]
+
+    for n in range(5, 9):
         loads[n].wait()
-    mass = slabs_of(mass_flat, mass_flat)
-    sign = jnp.where(row < 4, time_step, -time_step)
-    speeds = [
-        speed + (sign * mass[i]) * force[8 * i : 8 * i + 8, :] for i, speed in enumerate(slabs_of(flats.at[2], flats.at[3]))
-    ]
-    planes_to_flat(speeds, (fvn_ref, avn_ref), (rows_a, rows_b), lane1, row1)
-    moved = [u_ref[8 * i : 8 * i + 8, :] - sign * speeds[i] for i in range(4)]
-    planes_to_flat(moved, (fdn_ref, adn_ref), (rows_a, rows_b), lane1, row1)
-
-    pltpu.make_async_copy(recv, recv, part_recv).wait()
-    total = part[e]
-    for m in range(events - 1):
-        total = total + recv[m]
-    total_ref[...] = total
-    edges = [
-        pltpu.make_async_remote_copy(
-            total_ref, halo.at[n], edge_send.at[n], edge_recv.at[n], {"cuts": to}, MESH
+
+    def edges_of(n):
+        return [
+            pltpu.make_async_remote_copy(src, dst, edge_send.at[n, c], edge_recv.at[n, c], cut_at(m), MESH)
+            for c, (src, dst, m) in enumerate(
+                (
+                    (total_ref.at[n], halo.at[n, 0], 1),
+                    (total_ref.at[n], halo.at[n, 1], -1),
+                    (total_ref.at[n, pl.ds(16, 8)], halo_far.at[n, 0], 2),
+                    (total_ref.at[n, pl.ds(16, 8)], halo_far.at[n, 1], -2),
+                )
+            )
+        ]
+
+    def gathered(source, semaphore, n):
+        some = source.at[pl.ds(0, events - 1)]
+        pltpu.make_async_copy(some, some, semaphore).wait()
+        total = source[0]
+        for m in range(1, events):
+            total = total + source[m]
+        total_ref[n] = total
+        for copy in edges_of(n):
+            copy.start()
+
+    def smoothed(n):
+        for copy in edges_of(n):
+            copy.wait_recv()
+        parts = [halo[n, 0], total_ref[n], halo[n, 1]]
+        tall = jnp.concatenate(
+            [x[0:16, :] for x in parts] + [halo_far[n, 0]] + [x[16:24, :] for x in parts] + [halo_far[n, 1]],
+            axis=0,
         )
-        for n, to in enumerate((ahead, behind))
-    ]
-    for edge in edges:
-        edge.start()
-    for edge in edges:
-        edge.wait()
-    tall = lambda at: jnp.concatenate(
-        [halo[0, at : at + 16, :], total_ref[at : at + 16, :], halo[1, at : at + 16, :]], axis=0
-    )
-    along = jnp.dot(
-        band_ref[:, 0:48],
-        jnp.concatenate([tall(0), tall(16)], axis=1),
-        precision=lax.Precision.HIGHEST,
-        preferred_element_type=f32,
-    )
-    cols[e] = along[:, 0:128]
+        return jnp.dot(
+            band_ref[:, 0:88], tall, precision=lax.Precision.HIGHEST, preferred_element_type=f32
+        )
+
+    gathered(recv, part_recv, 0)
+
+    @pl.when(lead)
+    def _():
+        recv_short[e] = part[events]
+        gathered(recv_short, short_recv, 1)
+
+    cols[e] = smoothed(0)
     for m in range(1, events):
         pltpu.make_async_remote_copy(cols.at[e], cols.at[e], cols_send, cols_recv, event_at(m), MESH).start()
-    pltpu.make_async_copy(recv, recv, part_send).wait()
+    shorts = [
+        pltpu.make_async_remote_copy(lone, lone, lone_send.at[m], lone_recv, {"event": m}, MESH)
+        for m in range(events - 1)
+    ]
+
+    @pl.when(lead)
+    def _():
+        lone[...] = smoothed(1)
+        for copy in shorts:
+            copy.start()
+
+    @pl.when(jnp.logical_not(first))
+    def _():
+        force_ahead.wait_recv()
+        for f in range(2):
+            force[4 * f : 4 * f + 1, :] += carried[f : f + 1, :]
+
+    @pl.when(final)
+    def _():
+        force_back.wait_recv()
+        for i in range(4):
+            for f in range(2):
+                at = 8 * i + 4 * f + 3
+                force[at : at + 1, :] += returned[2 * i + f : 2 * i + f + 1, :]
+
+    ends = planes_to_flat(
+        [force[8 * i : 8 * i + 8, :] for i in range(4)], (rows_a, rows_b), lane1, row1
+    )
+    for f, (sign, now_out, speed_out) in enumerate(
+        ((time_step, fdn_ref, fvn_ref), (-time_step, adn_ref, avn_ref))
+    ):
+        rows = (rows_a, rows_b)[f]
+        for g in range(18):
+            at, size = 1024 * g, 1024 if g < 17 else 16
+            push = rows[8 * g : 8 * g + 8, :].reshape(1, 1024) if g < 17 else ends[f]
+            mass = run_of(mass_flat, at, size).reshape(1, size)
+            speed = flats[2 + f, 0:1, at : at + size] + (sign * mass) * push
+            speed_out[0:1, at : at + size] = speed
+            now_out[0:1, at : at + size] = flats[f, 0:1, at : at + size] - sign * speed
     some = cols.at[pl.ds(0, events - 1)]
     pltpu.make_async_copy(some, some, cols_recv).wait()
-    total = jnp.concatenate([cols[m] for m in range(events)] + [along[:, 128:256]], axis=1)
+    pl.when(jnp.logical_not(lead))(shorts[0].wait_recv)
+    total = jnp.concatenate([cols[m] for m in range(events)] + [lone[...]], axis=1)
     across = None
     for d in range(-cross_reach, cross_reach + 1):
         term = coef_ref[20 + d : 21 + d, :] * shifted(total, PZ * d)
@@ -509,6 +635,25 @@
         across = term if across is None else across + term
     sk_ref[...] = across[:, 0:PYZ]
     pltpu.make_async_copy(some, some, cols_send).wait()
+    seven = recv.at[pl.ds(0, events - 1)]
+    pltpu.make_async_copy(seven, seven, part_send).wait()
+    for copy in edges_of(0):
+        copy.wait_send()
+
+    @pl.when(lead)
+    def _():
+        for copy in edges_of(1) + shorts:
+            copy.wait_send()
+
+    pl.when(jnp.logical_not(lead))(short_part.wait_send)
+    pl.when(jnp.logical_not(first))(to_behind.wait_send)
+    pl.when(jnp.logical_not(final))(force_ahead.wait_send)
+    pl.when(first)(force_back.wait_send)
+
+    @pl.when(final)
+    def _():
+        planes_ahead.wait_send()
+        flux_ahead.wait_send()
 
 
 def store_kernel(a, b, c, d, k, a_hbm, b_hbm, c_hbm, d_hbm, k_hbm, sem):
@@ -548,7 +693,7 @@
                 big(56),
                 small(16),
                 big(32),
-                pltpu.VMEM((3, 624, 256), jnp.bfloat16),
+                pltpu.VMEM((2, 624, 256), jnp.bfloat16),
                 big(624),
                 big(40),
                 big(32),
@@ -557,25 +702,36 @@
                 big(32),
                 big(2),
                 big(8),
+                big(2),
+                big(8),
                 big(8),
                 big(2),
+                big(2),
+                big(8),
                 big(8),
                 big(8),
                 big(32),
                 big(32),
-                small(events, 32),
-                small(events - 1, 32),
-                small(32),
-                small(2, 32),
+                small(events + 1, 24),
+                small(events, 24),
+                small(events, 24),
+                small(2, 24),
+                small(2, 2, 24),
+                small(2, 2, 8),
                 small(events, 16),
+                small(16),
                 dma((9,)),
-                dma((3,)),
-                dma((3,)),
+                dma((5,)),
+                dma((5,)),
                 dma,
                 dma,
-                dma((2,)),
-                dma((2,)),
                 dma,
+                dma,
+                dma((2, 4)),
+                dma((2, 4)),
+                dma,
+                dma,
+                dma((events - 1,)),
                 dma,
             ],
             compiler_params=pltpu.CompilerParams(

time: 28.4 us -> 27.9 us (0.982)
  the two profiles are of different devices: /device:TPU:1 before, /device:TPU:8 now
where the time goes in v3:
time: 27.9 us; the launch traced here: 27.7 us
  Pallas kernels  26.4 us (95%)
  between operations  1.29 us (5%)
    pallas_call x1, Pallas kernels, run(): pl.pallas_call(functools.partial(step_kernel, events, slices), out_shape=...  25.7 us
    pallas_call x1, Pallas kernels, run(): pl.pallas_call(store_kernel, out_shape=(flat, flat, flat, flat, table), i...  0.77 us

profile of v3, /device:TPU:8, one launch (start us, length us, event | category | flops | bytes accessed | tf_op | source)
XLA Modules:
  0.0 27.7 jit_solution(10717631122289420925)
XLA Ops:
  1.3 25.7 %shard_map.137 = (f32[1,17424]{1,0:T(1,128)S(1)}, f32[1,17424]{1,0:T(1,128)S(1)}, f32[1,17424]{1,0:T(1,128)S(1)}, f32[1,17424]{1,0:T(1,128)S(1)}, f32[16,1089]{1,0:T(8,128)S(1)}) custom-call(f32[1,17424]{1,0:T(1,128)} %fd_hbm.1, f32[1,17424]{1,0:T(1,128)} %fv_hbm.1, f32[1,17424]{1,0:T(1,128)} %ad_hbm.1, f32[1,17424]{1,0:T(1,128)} %av_hbm.1, f32[17424]{0:T(1024)} %mass_hbm.1, ...), custom_call_target="tpu_custom_call" | custom-call | tf_op jit(solution)/shard_map/pallas_call | solution.py:679
  26.9 0.8 %shard_map.138 = (f32[1,17424]{1,0:T(1,128)}, f32[1,17424]{1,0:T(1,128)}, f32[1,17424]{1,0:T(1,128)}, f32[1,17424]{1,0:T(1,128)}, f32[16,1089]{1,0:T(8,128)}) custom-call(f32[1,17424]{1,0:T(1,128)S(1)} %get-tuple-element.10.a, f32[1,17424]{1,0:T(1,128)S(1)} %get-tuple-element.11.b, f32[1,17424]{1,0:T(1,128)S(1)} %get-tuple-element.12.c, ...), custom_call_target="tpu_custom_call" | custom-call | tf_op jit(solution)/shard_map/pallas_call | solution.py:746

commit v4 on v3

--- a/solution.py
+++ b/solution.py
@@ -78,8 +78,9 @@
     rows = table(np.arange(-PXU, 2 * PXU)).reshape(PXU, 3, 4, 4).transpose(0, 1, 3, 2).reshape(PXU, 48)
     places = PXU * np.arange(-2, 3)[:, None] + np.array([-4, -3, -2, -1, 16])[None, :]
     extra = np.pad(table(places.reshape(25)).reshape(PXU, 5, 5), ((0, 0), (0, 0), (0, 3)))
-    both = np.concatenate([rows, extra.reshape(PXU, 40)], axis=1)
-    return np.pad(-both, ((0, 0), (0, 40))).astype(np.float32)
+    wrapped = table((np.array([-4, -20, 12, 28])[:, None] + np.arange(5)[None, :]).reshape(20))
+    both = np.concatenate([rows, extra.reshape(PXU, 40), wrapped], axis=1)
+    return np.pad(-both, ((0, 0), (0, 20))).astype(np.float32)
 
 
 def shifted(x, step):
@@ -232,6 +233,12 @@
     halo_far,
     cols,
     lone,
+    wrap_rows,
+    wrap_extra,
+    wrap_terms,
+    wrap_total,
+    wrap_near,
+    wrap_sum,
     load_sem,
     halo_send,
     halo_recv,
@@ -245,22 +252,61 @@
     cols_recv,
     lone_send,
     lone_recv,
+    ready,
+    tile_send,
+    tile_recv,
+    extra_send,
+    extra_recv,
+    terms_send,
+    terms_recv,
+    near_send,
+    near_recv,
 ):
     f32 = jnp.float32
     e = lax.axis_index("event")
     s = lax.axis_index("cuts")
     first, final = s == 0, s == slices - 1
+    second, before_final = s == 1, s == slices - 2
     cut_at = lambda m: {"cuts": lax.rem(s + m + slices, slices)}
 
     barrier = pltpu.get_barrier_semaphore()
-    for m in (-1, 1, -2, 2):
+
+    def greet_cut(m):
         pl.semaphore_signal(barrier, inc=1, device_id=cut_at(m), device_id_type=MESH)
+
+    greet_cut(-1)
+    greet_cut(-2)
+    pl.when(jnp.logical_not(final))(lambda: greet_cut(1))
+    pl.when(s < slices - 2)(lambda: greet_cut(2))
 
     def event_at(m):
         return {"event": lax.rem(e + m, events)}
 
     for m in range(1, events):
         pl.semaphore_signal(barrier, inc=1, device_id=event_at(m), device_id_type=MESH)
+
+    def greet(cut):
+        for m in range(1, events):
+            to = {**event_at(m), "cuts": cut}
+            pl.semaphore_signal(barrier, inc=1, device_id=to, device_id_type=MESH)
+
+    @pl.when(first)
+    def _():
+        greet(slices - 1)
+        greet(slices - 2)
+
+
+    @pl.when(first)
+    def _():
+        for n in range(2):
+            halo[n, 0] = jnp.zeros((24, 128), jnp.float32)
+
+    @pl.when(s <= 1)
+    def _():
+        for n in range(2):
+            halo_far[n, 0] = jnp.zeros((8, 128), jnp.float32)
+
+    wrap_sum[...] = jnp.zeros((PXU, LANES), jnp.float32)
 
     loads = [
         pltpu.make_async_copy(src, dst, load_sem.at[n])
@@ -340,7 +386,15 @@
             at = 8 * i + 4 * f + 3
             stage_u[2 * i + f : 2 * i + f + 1, :] = u_ref[at : at + 1, :]
 
-    pl.semaphore_wait(barrier, events + 3)
+    more = (events - 1) * jnp.where(s >= slices - 2, 1, 0)
+    fewer = 2 * jnp.where(first, 1, 0) + jnp.where(second, 1, 0)
+    pl.semaphore_wait(barrier, events + 3 + more - fewer)
+
+    def tell(m):
+        pl.semaphore_signal(ready, inc=1, device_id=cut_at(m), device_id_type=MESH)
+
+    pl.when(final)(lambda: tell(1))
+    pl.when(s >= slices - 2)(lambda: tell(2))
     to_behind = pltpu.make_async_remote_copy(
         stage_g, ghost, halo_send.at[0], halo_recv.at[0], cut_at(-1), MESH
     )
@@ -483,19 +537,6 @@
                 part[m, 4 * i + 3 : 4 * i + 4, :] += terms[i][:, lanes]
             part[m, 20:21, :] = terms[4][:, lanes]
 
-    @pl.when(first)
-    def _():
-        plane = stage_g[...]
-        slopes = slopes_of(plane)
-        planes_ahead.wait_recv()
-        flux_ahead.wait_recv()
-        terms = last_terms(tail_u, tail_a, plane, slopes)
-        for m in range(events + 1):
-            lanes = slice(128 * m, 128 * m + 128)
-            part[m, 0:1, :] += terms[4][:, lanes]
-            for i in range(4):
-                part[m, 16 + i : 17 + i, :] = terms[i][:, lanes]
-
     lead = e == events - 1
     for m in range(1, events):
         to = event_at(m)
@@ -524,15 +565,6 @@
             for f in range(2):
                 at = 8 * i + 4 * f + 3
                 force[at : at + 1, :] += turned[i][f : f + 1, :]
-
-    @pl.when(first)
-    def _():
-        turned = last_force(tail_u, tail_a, stage_g[...])
-        for i in range(4):
-            stage_r[2 * i : 2 * i + 2, :] = turned[i]
-        force_back.start()
-        for f in range(2):
-            force[4 * f : 4 * f + 1, :] += turned[4][f : f + 1, :]
 
     for n in range(5, 9):
         loads[n].wait()
@@ -550,6 +582,30 @@
             )
         ]
 
+    def slot(n):
+        return e if n == 0 else events
+
+    def tiles_of(n):
+        return [
+            pltpu.make_async_remote_copy(
+                total_ref.at[n, pl.ds(0, 16)], wrap_rows.at[slot(n)], tile_send.at[n, m], tile_recv, {"event": m, "cuts": 0}, MESH
+            )
+            for m in range(events)
+        ]
+
+    def extras_of(n):
+        return [
+            pltpu.make_async_remote_copy(
+                total_ref.at[n, pl.ds(16, 8)],
+                wrap_extra.at[slot(n)],
+                extra_send.at[n, m],
+                extra_recv,
+                {"event": m, "cuts": 0},
+                MESH,
+            )
+            for m in range(events)
+        ]
+
     def gathered(source, semaphore, n):
         some = source.at[pl.ds(0, events - 1)]
         pltpu.make_async_copy(some, some, semaphore).wait()
@@ -557,12 +613,18 @@
         for m in range(1, events):
             total = total + source[m]
         total_ref[n] = total
-        for copy in edges_of(n):
-            copy.start()
+        ahead, behind, far_ahead, far_behind = edges_of(n)
+        pl.when(final)(lambda: [copy.start() for copy in tiles_of(n)] and None)
+        pl.when(before_final)(lambda: [copy.start() for copy in extras_of(n)] and None)
+        pl.when(jnp.logical_not(final))(ahead.start)
+        pl.when(s < slices - 2)(far_ahead.start)
 
     def smoothed(n):
-        for copy in edges_of(n):
-            copy.wait_recv()
+        ahead, behind, far_ahead, far_behind = edges_of(n)
+        behind.wait_recv()
+        far_behind.wait_recv()
+        pl.when(jnp.logical_not(first))(ahead.wait_recv)
+        pl.when(s > 1)(far_ahead.wait_recv)
         parts = [halo[n, 0], total_ref[n], halo[n, 1]]
         tall = jnp.concatenate(
             [x[0:16, :] for x in parts] + [halo_far[n, 0]] + [x[16:24, :] for x in parts] + [halo_far[n, 1]],
@@ -572,12 +634,22 @@
             band_ref[:, 0:88], tall, precision=lax.Precision.HIGHEST, preferred_element_type=f32
         )
 
+    def back_edges(n):
+        _, behind, _, far_behind = edges_of(n)
+        behind.start()
+        far_behind.start()
+
     gathered(recv, part_recv, 0)
 
     @pl.when(lead)
     def _():
         recv_short[e] = part[events]
         gathered(recv_short, short_recv, 1)
+
+    pl.when(first)(lambda: pl.semaphore_wait(ready, 2))
+    pl.when(second)(lambda: pl.semaphore_wait(ready, 1))
+    back_edges(0)
+    pl.when(lead)(lambda: back_edges(1))
 
     cols[e] = smoothed(0)
     for m in range(1, events):
@@ -592,6 +664,29 @@
         lone[...] = smoothed(1)
         for copy in shorts:
             copy.start()
+
+    @pl.when(first)
+    def _():
+        plane = stage_g[...]
+        slopes = slopes_of(plane)
+        planes_ahead.wait_recv()
+        flux_ahead.wait_recv()
+        terms = last_terms(tail_u, tail_a, plane, slopes)
+        for i in range(5):
+            wrap_terms[e, i : i + 1, :] = terms[i]
+        for m in range(1, events):
+            pltpu.make_async_remote_copy(
+                wrap_terms.at[e], wrap_terms.at[e], terms_send, terms_recv, event_at(m), MESH
+            ).start()
+
+    @pl.when(first)
+    def _():
+        turned = last_force(tail_u, tail_a, stage_g[...])
+        for i in range(4):
+            stage_r[2 * i : 2 * i + 2, :] = turned[i]
+        force_back.start()
+        for f in range(2):
+            force[4 * f : 4 * f + 1, :] += turned[4][f : f + 1, :]
 
     @pl.when(jnp.logical_not(first))
     def _():
@@ -621,10 +716,46 @@
             speed = flats[2 + f, 0:1, at : at + size] + (sign * mass) * push
             speed_out[0:1, at : at + size] = speed
             now_out[0:1, at : at + size] = flats[f, 0:1, at : at + size] - sign * speed
+    nears = [
+        pltpu.make_async_remote_copy(wrap_total, wrap_near, near_send.at[n], near_recv, cut_at(m), MESH)
+        for n, m in enumerate((1, -1, -2))
+    ]
+    table = band_ref[...]
+
+    def add(weights, rows):
+        wrap_sum[...] += jnp.dot(
+            weights, rows, precision=lax.Precision.HIGHEST, preferred_element_type=f32
+        )
+
+    def wide(ref, start, size):
+        return jnp.concatenate([ref[m, start : start + size, :] for m in range(events + 1)], axis=1)
+
+    @pl.when(first)
+    def _():
+        seven = wrap_terms.at[pl.ds(0, events - 1)]
+        pltpu.make_async_copy(seven, seven, terms_recv).wait()
+        total = wrap_terms[0]
+        for m in range(1, events):
+            total = total + wrap_terms[m]
+        wrap_total[...] = total
+        for copy in nears:
+            copy.start()
+        pltpu.make_async_copy(wrap_rows, wrap_rows, tile_recv).wait()
+        pltpu.make_async_copy(wrap_extra, wrap_extra, extra_recv).wait()
+        add(table[:, 88:93], total)
+        weights = jnp.concatenate([table[:, 0:16], table[:, 48:56]], axis=1)
+        add(weights, jnp.concatenate([wide(wrap_rows, 0, 16), wide(wrap_extra, 0, 8)], axis=0))
+
+    for n, place in enumerate((second, final, before_final)):
+        @pl.when(place)
+        def _():
+            nears[0].wait_recv()
+            add(table[:, 93 + 5 * n : 98 + 5 * n], wrap_near[...])
+
     some = cols.at[pl.ds(0, events - 1)]
     pltpu.make_async_copy(some, some, cols_recv).wait()
     pl.when(jnp.logical_not(lead))(shorts[0].wait_recv)
-    total = jnp.concatenate([cols[m] for m in range(events)] + [lone[...]], axis=1)
+    total = jnp.concatenate([cols[m] for m in range(events)] + [lone[...]], axis=1) + wrap_sum[...]
     across = None
     for d in range(-cross_reach, cross_reach + 1):
         term = coef_ref[20 + d : 21 + d, :] * shifted(total, PZ * d)
@@ -637,12 +768,29 @@
     pltpu.make_async_copy(some, some, cols_send).wait()
     seven = recv.at[pl.ds(0, events - 1)]
     pltpu.make_async_copy(seven, seven, part_send).wait()
-    for copy in edges_of(0):
-        copy.wait_send()
+
+    def sent(n):
+        ahead, behind, far_ahead, far_behind = edges_of(n)
+        behind.wait_send()
+        far_behind.wait_send()
+        pl.when(jnp.logical_not(final))(ahead.wait_send)
+        pl.when(s < slices - 2)(far_ahead.wait_send)
+        pl.when(final)(lambda: [copy.wait_send() for copy in tiles_of(n)] and None)
+        pl.when(before_final)(lambda: [copy.wait_send() for copy in extras_of(n)] and None)
+
+    sent(0)
 
     @pl.when(lead)
     def _():
-        for copy in edges_of(1) + shorts:
+        sent(1)
+        for copy in shorts:
+            copy.wait_send()
+
+    @pl.when(first)
+    def _():
+        seven = wrap_terms.at[pl.ds(0, events - 1)]
+        pltpu.make_async_copy(seven, seven, terms_send).wait()
+        for copy in nears:
             copy.wait_send()
 
     pl.when(jnp.logical_not(lead))(short_part.wait_send)
@@ -720,6 +868,12 @@
                 small(2, 2, 8),
                 small(events, 16),
                 small(16),
+                small(events + 1, 16),
+                small(events + 1, 8),
+                big(events, 5),
+                big(5),
+                big(5),
+                big(16),
                 dma((9,)),
                 dma((5,)),
                 dma((5,)),
@@ -732,6 +886,15 @@
                 dma,
                 dma,
                 dma((events - 1,)),
+                dma,
+                pltpu.SemaphoreType.REGULAR,
+                dma((2, events)),
+                dma,
+                dma((2, events)),
+                dma,
+                dma,
+                dma,
+                dma((3,)),
                 dma,
             ],
             compiler_params=pltpu.CompilerParams(

time: 27.9 us -> 26.9 us (0.964)
  the two profiles are of different devices: /device:TPU:8 before, /device:TPU:1 now
where the time goes in v4:
time: 26.9 us; the launch traced here: 26.8 us
  Pallas kernels  25.5 us (95%)
  between operations  1.29 us (5%)
    pallas_call x1, Pallas kernels, run(): pl.pallas_call(functools.partial(step_kernel, events, slices), out_shape=...  24.7 us
    pallas_call x1, Pallas kernels, run(): pl.pallas_call(store_kernel, out_shape=(flat, flat, flat, flat, table), i...  0.77 us

profile of v4, /device:TPU:1, one launch (start us, length us, event | category | flops | bytes accessed | tf_op | source)
XLA Modules:
  0.0 26.8 jit_solution(1752776585295456225)
XLA Ops:
  1.3 24.7 %shard_map.137 = (f32[1,17424]{1,0:T(1,128)S(1)}, f32[1,17424]{1,0:T(1,128)S(1)}, f32[1,17424]{1,0:T(1,128)S(1)}, f32[1,17424]{1,0:T(1,128)S(1)}, f32[16,1089]{1,0:T(8,128)S(1)}) custom-call(f32[1,17424]{1,0:T(1,128)} %fd_hbm.1, f32[1,17424]{1,0:T(1,128)} %fv_hbm.1, f32[1,17424]{1,0:T(1,128)} %ad_hbm.1, f32[1,17424]{1,0:T(1,128)} %av_hbm.1, f32[17424]{0:T(1024)} %mass_hbm.1, ...), custom_call_target="tpu_custom_call" | custom-call | tf_op jit(solution)/shard_map/pallas_call | solution.py:827
  26.0 0.8 %shard_map.138 = (f32[1,17424]{1,0:T(1,128)}, f32[1,17424]{1,0:T(1,128)}, f32[1,17424]{1,0:T(1,128)}, f32[1,17424]{1,0:T(1,128)}, f32[16,1089]{1,0:T(8,128)}) custom-call(f32[1,17424]{1,0:T(1,128)S(1)} %get-tuple-element.10.a, f32[1,17424]{1,0:T(1,128)S(1)} %get-tuple-element.11.b, f32[1,17424]{1,0:T(1,128)S(1)} %get-tuple-element.12.c, ...), custom_call_target="tpu_custom_call" | custom-call | tf_op jit(solution)/shard_map/pallas_call | solution.py:909

commit v5 on v4

--- a/solution.py
+++ b/solution.py
@@ -232,7 +232,6 @@
     halo,
     halo_far,
     cols,
-    lone,
     wrap_rows,
     wrap_extra,
     wrap_terms,
@@ -251,7 +250,6 @@
     cols_send,
     cols_recv,
     lone_send,
-    lone_recv,
     ready,
     tile_send,
     tile_recv,
@@ -282,7 +280,8 @@
     def event_at(m):
         return {"event": lax.rem(e + m, events)}
 
-    for m in range(1, events):
+    order = sorted(range(1, events), key=lambda m: abs(m - events // 2))
+    for m in order:
         pl.semaphore_signal(barrier, inc=1, device_id=event_at(m), device_id_type=MESH)
 
     def greet(cut):
@@ -588,9 +587,9 @@
     def tiles_of(n):
         return [
             pltpu.make_async_remote_copy(
-                total_ref.at[n, pl.ds(0, 16)], wrap_rows.at[slot(n)], tile_send.at[n, m], tile_recv, {"event": m, "cuts": 0}, MESH
+                total_ref.at[n, pl.ds(0, 16)], wrap_rows.at[slot(n)], tile_send.at[n, m], tile_recv, {**event_at(m), "cuts": 0}, MESH
             )
-            for m in range(events)
+            for m in order + [0]
         ]
 
     def extras_of(n):
@@ -600,10 +599,10 @@
                 wrap_extra.at[slot(n)],
                 extra_send.at[n, m],
                 extra_recv,
-                {"event": m, "cuts": 0},
+                {**event_at(m), "cuts": 0},
                 MESH,
             )
-            for m in range(events)
+            for m in order + [0]
         ]
 
     def gathered(source, semaphore, n):
@@ -631,7 +630,7 @@
             axis=0,
         )
         return jnp.dot(
-            band_ref[:, 0:88], tall, precision=lax.Precision.HIGHEST, preferred_element_type=f32
+            band_ref[:, 0:88], tall, precision=lax.Precision.HIGH, preferred_element_type=f32
         )
 
     def back_edges(n):
@@ -652,18 +651,30 @@
     pl.when(lead)(lambda: back_edges(1))
 
     cols[e] = smoothed(0)
-    for m in range(1, events):
-        pltpu.make_async_remote_copy(cols.at[e], cols.at[e], cols_send, cols_recv, event_at(m), MESH).start()
-    shorts = [
-        pltpu.make_async_remote_copy(lone, lone, lone_send.at[m], lone_recv, {"event": m}, MESH)
+    pairs = [
+        pltpu.make_async_remote_copy(
+            cols.at[pl.ds(events - 1, 2)],
+            cols.at[pl.ds(events - 1, 2)],
+            lone_send.at[m],
+            cols_recv,
+            {"event": m},
+            MESH,
+        )
         for m in range(events - 1)
     ]
 
     @pl.when(lead)
     def _():
-        lone[...] = smoothed(1)
-        for copy in shorts:
+        cols[events] = smoothed(1)
+        for copy in pairs:
             copy.start()
+
+    @pl.when(jnp.logical_not(lead))
+    def _():
+        for m in range(1, events):
+            pltpu.make_async_remote_copy(
+                cols.at[e], cols.at[e], cols_send, cols_recv, event_at(m), MESH
+            ).start()
 
     @pl.when(first)
     def _():
@@ -724,7 +735,7 @@
 
     def add(weights, rows):
         wrap_sum[...] += jnp.dot(
-            weights, rows, precision=lax.Precision.HIGHEST, preferred_element_type=f32
+            weights, rows, precision=lax.Precision.HIGH, preferred_element_type=f32
         )
 
     def wide(ref, start, size):
@@ -752,10 +763,13 @@
             nears[0].wait_recv()
             add(table[:, 93 + 5 * n : 98 + 5 * n], wrap_near[...])
 
-    some = cols.at[pl.ds(0, events - 1)]
-    pltpu.make_async_copy(some, some, cols_recv).wait()
-    pl.when(jnp.logical_not(lead))(shorts[0].wait_recv)
-    total = jnp.concatenate([cols[m] for m in range(events)] + [lone[...]], axis=1) + wrap_sum[...]
+    def got(count, semaphore):
+        some = cols.at[pl.ds(0, count)]
+        pltpu.make_async_copy(some, some, semaphore).wait()
+
+    pl.when(lead)(lambda: got(events - 1, cols_recv))
+    pl.when(jnp.logical_not(lead))(lambda: got(events, cols_recv))
+    total = jnp.concatenate([cols[m] for m in range(events + 1)], axis=1) + wrap_sum[...]
     across = None
     for d in range(-cross_reach, cross_reach + 1):
         term = coef_ref[20 + d : 21 + d, :] * shifted(total, PZ * d)
@@ -765,7 +779,7 @@
         term = coef_ref[29 + d : 30 + d, :] * shifted(total, d)
         across = term if across is None else across + term
     sk_ref[...] = across[:, 0:PYZ]
-    pltpu.make_async_copy(some, some, cols_send).wait()
+    pl.when(jnp.logical_not(lead))(lambda: got(events - 1, cols_send))
     seven = recv.at[pl.ds(0, events - 1)]
     pltpu.make_async_copy(seven, seven, part_send).wait()
 
@@ -783,7 +797,7 @@
     @pl.when(lead)
     def _():
         sent(1)
-        for copy in shorts:
+        for copy in pairs:
             copy.wait_send()
 
     @pl.when(first)
@@ -866,8 +880,7 @@
                 small(2, 24),
                 small(2, 2, 24),
                 small(2, 2, 8),
-                small(events, 16),
-                small(16),
+                small(events + 1, 16),
                 small(events + 1, 16),
                 small(events + 1, 8),
                 big(events, 5),
@@ -886,7 +899,6 @@
                 dma,
                 dma,
                 dma((events - 1,)),
-                dma,
                 pltpu.SemaphoreType.REGULAR,
                 dma((2, events)),
                 dma,

time: 26.9 us -> 26.8 us (level)
  no operation moved by 1% of the time
where the time goes in v5:
time: 26.8 us; the launch traced here: 26.7 us
  Pallas kernels  25.4 us (95%)
  between operations  1.29 us (5%)
    pallas_call x1, Pallas kernels, run(): pl.pallas_call(functools.partial(step_kernel, events, slices), out_shape=...  24.6 us
    pallas_call x1, Pallas kernels, run(): pl.pallas_call(store_kernel, out_shape=(flat, flat, flat, flat, table), i...  0.77 us

profile of v5, /device:TPU:1, one launch (start us, length us, event | category | flops | bytes accessed | tf_op | source)
XLA Modules:
  0.0 26.7 jit_solution(12989928262624174415)
XLA Ops:
  1.3 24.6 %shard_map.137 = (f32[1,17424]{1,0:T(1,128)S(1)}, f32[1,17424]{1,0:T(1,128)S(1)}, f32[1,17424]{1,0:T(1,128)S(1)}, f32[1,17424]{1,0:T(1,128)S(1)}, f32[16,1089]{1,0:T(8,128)S(1)}) custom-call(f32[1,17424]{1,0:T(1,128)} %fd_hbm.1, f32[1,17424]{1,0:T(1,128)} %fv_hbm.1, f32[1,17424]{1,0:T(1,128)} %ad_hbm.1, f32[1,17424]{1,0:T(1,128)} %av_hbm.1, f32[17424]{0:T(1024)} %mass_hbm.1, ...), custom_call_target="tpu_custom_call" | custom-call | tf_op jit(solution)/shard_map/pallas_call | solution.py:841
  25.9 0.8 %shard_map.138 = (f32[1,17424]{1,0:T(1,128)}, f32[1,17424]{1,0:T(1,128)}, f32[1,17424]{1,0:T(1,128)}, f32[1,17424]{1,0:T(1,128)}, f32[16,1089]{1,0:T(8,128)}) custom-call(f32[1,17424]{1,0:T(1,128)S(1)} %get-tuple-element.10.a, f32[1,17424]{1,0:T(1,128)S(1)} %get-tuple-element.11.b, f32[1,17424]{1,0:T(1,128)S(1)} %get-tuple-element.12.c, ...), custom_call_target="tpu_custom_call" | custom-call | tf_op jit(solution)/shard_map/pallas_call | solution.py:921

commit v6 on v5

--- a/solution.py
+++ b/solution.py
@@ -537,7 +537,7 @@
             part[m, 20:21, :] = terms[4][:, lanes]
 
     lead = e == events - 1
-    for m in range(1, events):
+    for m in order:
         to = event_at(m)
         pltpu.make_async_remote_copy(
             part.at[to["event"]], recv.at[e], part_send, part_recv, to, MESH
@@ -671,7 +671,7 @@
 
     @pl.when(jnp.logical_not(lead))
     def _():
-        for m in range(1, events):
+        for m in order:
             pltpu.make_async_remote_copy(
                 cols.at[e], cols.at[e], cols_send, cols_recv, event_at(m), MESH
             ).start()
@@ -685,7 +685,7 @@
         terms = last_terms(tail_u, tail_a, plane, slopes)
         for i in range(5):
             wrap_terms[e, i : i + 1, :] = terms[i]
-        for m in range(1, events):
+        for m in order:
             pltpu.make_async_remote_copy(
                 wrap_terms.at[e], wrap_terms.at[e], terms_send, terms_recv, event_at(m), MESH
             ).start()

time: 26.8 us -> 27.5 us (1.026)
  Pallas kernels: 25.4 us -> 26.1 us
    pallas_call x1, Pallas kernels: 24.6 us -> 25.3 us  [run(): pl.pallas_call(functools.partial(step_kernel, events, slices), out_shape=...]
where the time goes in v6:
time: 27.5 us; the launch traced here: 27.4 us
  Pallas kernels  26.1 us (95%)
  between operations  1.29 us (5%)
    pallas_call x1, Pallas kernels, run(): pl.pallas_call(functools.partial(step_kernel, events, slices), out_shape=...  25.3 us
    pallas_call x1, Pallas kernels, run(): pl.pallas_call(store_kernel, out_shape=(flat, flat, flat, flat, table), i...  0.77 us

profile of v6, /device:TPU:1, one launch (start us, length us, event | category | flops | bytes accessed | tf_op | source)
XLA Modules:
  0.0 27.4 jit_solution(8883048171785692359)
XLA Ops:
  1.3 25.3 %shard_map.137 = (f32[1,17424]{1,0:T(1,128)S(1)}, f32[1,17424]{1,0:T(1,128)S(1)}, f32[1,17424]{1,0:T(1,128)S(1)}, f32[1,17424]{1,0:T(1,128)S(1)}, f32[16,1089]{1,0:T(8,128)S(1)}) custom-call(f32[1,17424]{1,0:T(1,128)} %fd_hbm.1, f32[1,17424]{1,0:T(1,128)} %fv_hbm.1, f32[1,17424]{1,0:T(1,128)} %ad_hbm.1, f32[1,17424]{1,0:T(1,128)} %av_hbm.1, f32[17424]{0:T(1024)} %mass_hbm.1, ...), custom_call_target="tpu_custom_call" | custom-call | tf_op jit(solution)/shard_map/pallas_call | solution.py:841
  26.6 0.8 %shard_map.138 = (f32[1,17424]{1,0:T(1,128)}, f32[1,17424]{1,0:T(1,128)}, f32[1,17424]{1,0:T(1,128)}, f32[1,17424]{1,0:T(1,128)}, f32[16,1089]{1,0:T(8,128)}) custom-call(f32[1,17424]{1,0:T(1,128)S(1)} %get-tuple-element.10.a, f32[1,17424]{1,0:T(1,128)S(1)} %get-tuple-element.11.b, f32[1,17424]{1,0:T(1,128)S(1)} %get-tuple-element.12.c, ...), custom_call_target="tpu_custom_call" | custom-call | tf_op jit(solution)/shard_map/pallas_call | solution.py:921
